TPU v7x, 32 devices: a whole 2x2x4 slice. The times are simulated.
32 devices in a mesh: grp: 8 (over y, x, core), sub: 4 (over z).
Axes of the slice: x: 2, y: 2, z: 4, core: 2. Of those that a mesh axis runs over, the one named last changes fastest.
Arguments:
- basis: bfloat16 [8, 4, 270, 1152], P('grp', 'sub'), may hold values from -6 to 6
- stiffness: bfloat16 [8, 4, 1152, 1152], P('grp', 'sub'), may hold values from -0.1875 to 0.1875
- inverse: bfloat16 [8, 4, 1152, 1152], P('grp', 'sub'), may hold values from -0.1875 to 0.1875
- coupling: bfloat16 [8, 4, 4, 768, 1152], P('grp', 'sub'), may hold values from -0.109375 to 0.109375
- panel_index: int32 [8, 4, 4, 6], P('grp', 'sub'), may hold values from 0 to 8, as said below
- panel_count: int32 [8, 4, 4], P('grp', 'sub'), may hold values from 1 to 6, as said below
- owner_map: int32 [8, 4, 270], P('grp', 'sub'), may hold values from 0 to 255, as said below
Outputs:
- coarse_matrix: float32 [256, 256], P(('grp', 'sub'))
Inputs may be any that keep to these rules, and one draw needn't show every extreme that they name: `panel_index`: in every draw some slot names panel 9 - 1 and some names panel 0. `panel_count`: in every draw some direction has 6 live slots and some has one. Subdomain (g, s) owns the rows b * 8 to b * 8 + 7 of coarse_matrix with b = g * 4 + s; entries of owner_map may name any column, repeats allowed; column 0 and column 256 - 1 are named in every draw.
All inputs are finite; a program needn't handle non-finite values.
Results may differ from a plain program's by a relative error of at most 0.0056.
Values may be sent and summed in bfloat16 or wider, within the bound.
No kernel may reach another device: no remote copies, remote signals or barrier semaphores. Data moves between devices by JAX's collectives and lax.ppermute only.
A program may use at most 128 MiB of HBM per device.

v0:
```python
import jax
import jax.numpy as jnp
from jax import lax
from jax.sharding import PartitionSpec as P

K = 270
PANEL = 128
NB = 9
CMAX = 6
OWN = 8


def extended(block, sides, width):
    for axis, dim in sides:
        count = lax.axis_size(axis)
        forward = [(i, i + 1) for i in range(count - 1)]
        backward = [(target, source) for source, target in forward]
        low = lax.ppermute(
            lax.slice_in_dim(block, block.shape[dim] - width, None, axis=dim), axis, forward
        )
        high = lax.ppermute(lax.slice_in_dim(block, 0, width, axis=dim), axis, backward)
        block = jnp.concatenate([low, block, high], axis=dim)
    return block


def live_slots(values, live_count):
    alive_mask = (jnp.arange(CMAX) < live_count).astype(values.dtype)
    return values * alive_mask[None, :, None]


def select_panels(values, panel_ids):
    panels = values.reshape(K, NB, PANEL)
    picker = (panel_ids[:, None] == jnp.arange(NB, dtype=jnp.int32)[None, :]).astype(jnp.bfloat16)
    chosen = jnp.einsum("knp,cn->kcp", panels, picker, preferred_element_type=jnp.float32)
    return chosen.astype(jnp.bfloat16)


def pick_panels(values, panel_ids, live_count):
    return live_slots(select_panels(values, panel_ids), live_count)


def spread_block(coarse, rows_at, cols_at, columns_all):
    positions = jnp.arange(columns_all, dtype=jnp.int32)
    row_table = (rows_at[:, None] == positions[None, :]).astype(jnp.float32)
    col_table = (cols_at[:, None] == positions[None, :]).astype(jnp.float32)
    placed_rows = lax.dot_general(
        row_table,
        coarse,
        (((0,), (0,)), ((), ())),
        precision=lax.Precision.HIGHEST,
        preferred_element_type=jnp.float32,
    )
    return jnp.dot(
        placed_rows, col_table, precision=lax.Precision.HIGHEST, preferred_element_type=jnp.float32
    )


def shards(basis, stiffness, inverse, coupling, panel_index, panel_count, owner_map):
    basis_local = basis[0, 0]
    stiffness_local = stiffness[0, 0]
    inverse_local = inverse[0, 0]
    coupling_local = coupling[0, 0]
    index_local = panel_index[0, 0]
    count_local = panel_count[0, 0]
    owner_local = owner_map[0, 0]
    rows_device = NB * PANEL
    slot_width = CMAX * PANEL
    grp_side = extended(basis_local, (("grp", 1),), rows_device)
    sub_side = extended(basis_local, (("sub", 1),), rows_device)
    sources = [
        grp_side[:, :rows_device],
        grp_side[:, 2 * rows_device :],
        sub_side[:, :rows_device],
        sub_side[:, 2 * rows_device :],
    ]
    picked = [
        pick_panels(sources[direction], index_local[direction], count_local[direction])
        for direction in range(4)
    ]
    rows_margin = jnp.stack(picked, axis=1).reshape(K, 4 * slot_width)
    margin = jnp.dot(
        rows_margin,
        coupling_local.reshape(4 * slot_width, rows_device),
        preferred_element_type=jnp.float32,
    ).astype(jnp.bfloat16)
    extension = (
        jnp.dot(basis_local, inverse_local, preferred_element_type=jnp.float32)
        + jnp.dot(margin, inverse_local, preferred_element_type=jnp.float32)
    ).astype(jnp.bfloat16)
    projected = jnp.dot(extension, stiffness_local, preferred_element_type=jnp.float32).astype(
        jnp.bfloat16
    )
    scale_factor = float(NB * PANEL * K) ** (-0.5)
    coarse = jnp.dot(projected, extension.T, preferred_element_type=jnp.float32) * scale_factor
    group_count = lax.axis_size("grp")
    member_count = lax.axis_size("sub")
    columns_all = OWN * group_count * member_count
    owner_block = owner_local // OWN
    offset = owner_local % OWN
    row_place = (
        owner_block % member_count * group_count + owner_block // member_count
    ) * OWN + offset
    contributions = spread_block(coarse, row_place, owner_local, columns_all)
    sectioned = lax.psum_scatter(contributions, "sub", scatter_dimension=0, tiled=True)
    owned_block = lax.psum_scatter(sectioned, "grp", scatter_dimension=0, tiled=True)
    return owned_block


def solution(mesh):
    in_specs = (
        P("grp", "sub", None, None),
        P("grp", "sub", None, None),
        P("grp", "sub", None, None),
        P("grp", "sub", None, None, None),
        P("grp", "sub", None, None),
        P("grp", "sub", None),
        P("grp", "sub", None),
    )
    out_specs = P(("grp", "sub"), None)
    return jax.shard_map(shards, mesh=mesh, in_specs=in_specs, out_specs=out_specs, check_vma=False)
```

profile of v0, /device:TPU:0, one launch (start us, length us, event | category | flops | bytes accessed | tf_op | source)
XLA Modules:
  0.0 132.9 jit_solution(15054278289783646318)
XLA Ops:
  6.5 3.5 %collective-permute-start = (bf16[270,1152]{1,0:T(8,128)(2,1)}, bf16[270,1152]{1,0:T(8,128)(2,1)}, u32[]{:S(2)}, u32[]{:S(2)}) collective-permute-start(bf16[270,1152]{1,0:T(8,128)(2,1)} %bitcast.77), channel_id=1, source_target_pairs={{0,4},{4,8},{8,12},{12,16},{16,20},{20,24},{24,28},{1,5},{5,9},{9,... | collective-permute-start | bytes 1866248 | tf_op jit(solution)/shard_map/ppermute | solution.py:18
  10.0 1.3 collective-permute-start.1
  11.3 5.1 %collective-permute-start.2 = (bf16[270,1152]{1,0:T(8,128)(2,1)}, bf16[270,1152]{1,0:T(8,128)(2,1)}, u32[]{:S(2)}, u32[]{:S(2)}) collective-permute-start(bf16[270,1152]{1,0:T(8,128)(2,1)} %bitcast.79), channel_id=1, source_target_pairs={{0,1},{1,2},{2,3},{4,5},{5,6},{6,7},{8,9},{9,10},{10,11},{12,13},{... | collective-permute-start | bytes 1866248 | tf_op jit(solution)/shard_map/ppermute | solution.py:18
  16.5 1.3 collective-permute-start.3
  17.8 1.5 %fusion.45 = (s32[1,1,1]{2,1,0:T(1,128)}, s32[1,1,1]{2,1,0:T(1,128)}, s32[1,1,1]{2,1,0:T(1,128)}, s32[1,1,1]{2,1,0:T(1,128)}) fusion(s32[1,1,4]{2,1,0:T(1,128)} %param.12), kind=kLoop, calls=%fused_computation.69 | loop fusion | bytes 32 | tf_op jit(solution)/shard_map/slice | solution.py:77
  20.3 1.4 %slice_bitcast_fusion.3 = (s32[6]{0:T(128)}, s32[6]{0:T(128)}, s32[6]{0:T(128)S(1)}, s32[6]{0:T(128)S(1)}) fusion(s32[1,1,4,6]{3,2,1,0:T(4,128)} %param.11), kind=kLoop, calls=%fused_computation.67 | loop fusion | bytes 192 | tf_op jit(solution)/shard_map/eq | solution.py:33
  22.9 1.2 compare_convert_fusion.1
  24.8 1.1 compare_convert_fusion
  26.0 3.2 %fusion.3 = f32[270,1152]{1,0:T(8,128)} fusion(bf16[1,1,1152,1152]{3,2,1,0:T(8,128)(2,1)S(1)} %copy-done, bf16[1,1,270,1152]{3,2,1,0:T(8,128)(2,1)} %param.7), kind=kOutput, calls=%fused_computation.4 | convolution fusion | flops 716636160 | bytes 4520448 | tf_op jit(solution)/shard_map/dot_general | solution.py:87
  29.2 1.5 %copy.8 = bf16[270,1152]{0,1:T(8,128)(2,1)S(1)} copy(bf16[270,1152]{1,0:T(8,128)(2,1)} %collective-permute-done) | data formatting | bytes 1244160 | tf_op jit(solution)/shard_map/ppermute | solution.py:18
  30.7 1.9 %copy.9 = bf16[270,9,128]{2,1,0:T(8,128)(2,1)} copy(bf16[270,9,128]{0,2,1:T(8,128)(2,1)S(1)} %bitcast.72) | data formatting | bytes 1244160 | tf_op jit(solution)/shard_map/reshape | solution.py:32
  32.6 1.5 %copy.10 = bf16[270,1152]{0,1:T(8,128)(2,1)S(1)} copy(bf16[270,1152]{1,0:T(8,128)(2,1)} %collective-permute-done.1) | data formatting | bytes 1244160 | tf_op jit(solution)/shard_map/ppermute | solution.py:21
  34.1 1.9 %copy.11 = bf16[270,9,128]{2,1,0:T(8,128)(2,1)} copy(bf16[270,9,128]{0,2,1:T(8,128)(2,1)S(1)} %bitcast.73) | data formatting | bytes 1244160 | tf_op jit(solution)/shard_map/reshape | solution.py:32
  36.0 1.5 %copy.12 = bf16[270,1152]{0,1:T(8,128)(2,1)S(1)} copy(bf16[270,1152]{1,0:T(8,128)(2,1)} %collective-permute-done.2) | data formatting | bytes 1244160 | tf_op jit(solution)/shard_map/ppermute | solution.py:18
  37.5 1.9 %copy.13 = bf16[270,9,128]{2,1,0:T(8,128)(2,1)} copy(bf16[270,9,128]{0,2,1:T(8,128)(2,1)S(1)} %bitcast.74) | data formatting | bytes 1244160 | tf_op jit(solution)/shard_map/reshape | solution.py:32
  39.4 1.5 %copy.14 = bf16[270,1152]{0,1:T(8,128)(2,1)S(1)} copy(bf16[270,1152]{1,0:T(8,128)(2,1)} %collective-permute-done.3) | data formatting | bytes 1244160 | tf_op jit(solution)/shard_map/ppermute | solution.py:21
  40.9 1.9 %copy.15 = bf16[270,9,128]{2,1,0:T(8,128)(2,1)} copy(bf16[270,9,128]{0,2,1:T(8,128)(2,1)S(1)} %bitcast.75) | data formatting | bytes 1244160 | tf_op jit(solution)/shard_map/reshape | solution.py:32
  42.9 1.8 %fusion.12 = bf16[270,1,6,128]{3,2,0,1:T(8,128)(2,1)S(1)} fusion(bf16[270,9,128]{2,1,0:T(8,128)(2,1)} %copy.9, bf16[6]{0:T(256)(128)(2,1)} %compare_convert_fusion.3, s32[6]{0:T(128)} %get-tuple-element.5), kind=kOutput, calls=%fused_computation.15 | convolution fusion | flops 4147254 | bytes 1036836 | tf_op jit(solution)/shard_map/knp,cn->kcp/dot_general | solution.py:34
  47.2 1.7 %copy.16 = bf16[270,4,6,128]{3,2,1,0:T(8,128)(2,1)} copy(bf16[270,4,6,128]{3,2,0,1:T(8,128)(2,1)S(1)} %pad_maximum_fusion) | data formatting | bytes 3317760 | tf_op jit(solution)/shard_map/stack | solution.py:80
  48.9 4.4 %reshape.138 = bf16[270,3072]{1,0:T(8,128)(2,1)} reshape(bf16[270,4,6,128]{3,2,1,0:T(8,128)(2,1)} %copy.16) | data formatting | bytes 3317760 | tf_op jit(solution)/shard_map/reshape | solution.py:80
  53.3 8.4 %fusion.8 = bf16[270,1152]{1,0:T(8,128)(2,1)} fusion(f32[270,1152]{1,0:T(8,128)} %fusion.3, bf16[1,1,1152,1152]{3,2,1,0:T(8,128)(2,1)S(1)} %copy-done, bf16[270,3072]{1,0:T(8,128)(2,1)} %reshape.138, bf16[3072,1152]{1,0:T(8,128)(2,1)} %bitcast.76), kind=kOutput, calls=%fused_computation.8 | convolution fusion | flops 2628599040 | bytes 13257216 | tf_op jit(solution)/shard_map/dot_general | solution.py:88
  61.7 3.5 %convolution_multiply_fusion = f32[270,270]{1,0:T(8,128)S(1)} fusion(bf16[270,1152]{1,0:T(8,128)(2,1)} %fusion.8, bf16[1,1,1152,1152]{3,2,1,0:T(8,128)(2,1)} %param.8), kind=kOutput, calls=%fused_computation.22 | convolution fusion | flops 884981696 | bytes 3567888 | tf_op jit(solution)/shard_map/dot_general | solution.py:94
  67.1 24.2 %reduce-scatter.3.cloned.1.call-done = f32[64,256]{1,0:T(8,128)} async-done(((f32[256,256]{1,0:T(8,128)}), f32[64,256]{1,0:T(8,128)}) %reduce-scatter.3.cloned.1.call-update) | async-done | bytes 65552 | tf_op jit(solution)/shard_map/reduce_scatter | solution.py:104
  91.3 34.8 %reduce-scatter.5.cloned.1.call-done = f32[8,256]{1,0:T(8,128)} async-done(((f32[64,256]{1,0:T(8,128)}), f32[8,256]{1,0:T(8,128)}) %reduce-scatter.5.cloned.1.call-update) | async-done | bytes 8208 | tf_op jit(solution)/shard_map/reduce_scatter | solution.py:105
  (30 shorter events, 7.3 us)
Async XLA Ops:
  6.5 19.4 %copy-start = (bf16[1,1,1152,1152]{3,2,1,0:T(8,128)(2,1)S(1)}, bf16[1,1,1152,1152]{3,2,1,0:T(8,128)(2,1)}, u32[]{:S(2)}) copy-start(bf16[1,1,1152,1152]{3,2,1,0:T(8,128)(2,1)} %param.9) | copy-start | bytes 7962628
  6.5 84.7 %reduce-scatter.3.cloned.1.call-start = ((), (), s32[]{:S(2)}) async-start(), calls=%async_computation.2 | async-start | bytes 327680 | tf_op jit(solution)/shard_map/reduce_scatter | solution.py:104
  6.5 22.6 %collective-permute-start = (bf16[270,1152]{1,0:T(8,128)(2,1)}, bf16[270,1152]{1,0:T(8,128)(2,1)}, u32[]{:S(2)}, u32[]{:S(2)}) collective-permute-start(bf16[270,1152]{1,0:T(8,128)(2,1)} %bitcast.77), channel_id=1, source_target_pairs={{0,4},{4,8},{8,12},{12,16},{16,20},{20,24},{24,28},{1,5},{5,9},{9,... | collective-permute-start | bytes 1866248 | tf_op jit(solution)/shard_map/ppermute | solution.py:18
  10.0 22.5 %collective-permute-start.1 = (bf16[270,1152]{1,0:T(8,128)(2,1)}, bf16[270,1152]{1,0:T(8,128)(2,1)}, u32[]{:S(2)}, u32[]{:S(2)}) collective-permute-start(bf16[270,1152]{1,0:T(8,128)(2,1)} %bitcast.78), channel_id=1, source_target_pairs={{4,0},{8,4},{12,8},{16,12},{20,16},{24,20},{28,24},{5,1},{9,5},{13... | collective-permute-start | bytes 1866248 | tf_op jit(solution)/shard_map/ppermute | solution.py:21
  11.3 24.7 %collective-permute-start.2 = (bf16[270,1152]{1,0:T(8,128)(2,1)}, bf16[270,1152]{1,0:T(8,128)(2,1)}, u32[]{:S(2)}, u32[]{:S(2)}) collective-permute-start(bf16[270,1152]{1,0:T(8,128)(2,1)} %bitcast.79), channel_id=1, source_target_pairs={{0,1},{1,2},{2,3},{4,5},{5,6},{6,7},{8,9},{9,10},{10,11},{12,13},{... | collective-permute-start | bytes 1866248 | tf_op jit(solution)/shard_map/ppermute | solution.py:18
  16.5 22.9 %collective-permute-start.3 = (bf16[270,1152]{1,0:T(8,128)(2,1)}, bf16[270,1152]{1,0:T(8,128)(2,1)}, u32[]{:S(2)}, u32[]{:S(2)}) collective-permute-start(bf16[270,1152]{1,0:T(8,128)(2,1)} %bitcast.80), channel_id=1, source_target_pairs={{1,0},{2,1},{3,2},{5,4},{6,5},{7,6},{9,8},{10,9},{11,10},{13,12},{... | collective-permute-start | bytes 1866248 | tf_op jit(solution)/shard_map/ppermute | solution.py:21
  42.9 1.8 %copy-start.1 = (bf16[270,9,128]{2,1,0:T(8,128)(2,1)S(1)}, bf16[270,9,128]{2,1,0:T(8,128)(2,1)}, u32[]{:S(2)}) copy-start(bf16[270,9,128]{2,1,0:T(8,128)(2,1)} %copy.11) | copy-start | bytes 1866244
  42.9 2.9 %copy-start.2 = (bf16[270,9,128]{2,1,0:T(8,128)(2,1)S(1)}, bf16[270,9,128]{2,1,0:T(8,128)(2,1)}, u32[]{:S(2)}) copy-start(bf16[270,9,128]{2,1,0:T(8,128)(2,1)} %copy.13) | copy-start | bytes 1866244
  42.9 2.9 %copy-start.4 = (bf16[6]{0:T(256)(128)(2,1)S(1)}, bf16[6]{0:T(256)(128)(2,1)}, u32[]{:S(2)}) copy-start(bf16[6]{0:T(256)(128)(2,1)} %compare_convert_fusion.1) | copy-start | bytes 40
  44.6 1.5 %copy-start.3 = (bf16[270,9,128]{2,1,0:T(8,128)(2,1)S(1)}, bf16[270,9,128]{2,1,0:T(8,128)(2,1)}, u32[]{:S(2)}) copy-start(bf16[270,9,128]{2,1,0:T(8,128)(2,1)} %copy.15) | copy-start | bytes 1866244
  44.6 1.5 %copy-start.5 = (bf16[6]{0:T(256)(128)(2,1)S(1)}, bf16[6]{0:T(256)(128)(2,1)}, u32[]{:S(2)}) copy-start(bf16[6]{0:T(256)(128)(2,1)} %compare_convert_fusion) | copy-start | bytes 40
  67.1 59.0 %reduce-scatter.5.cloned.1.call-start = ((), (), s32[]{:S(2)}) async-start(), calls=%async_computation.3 | async-start | bytes 73728 | tf_op jit(solution)/shard_map/reduce_scatter | solution.py:105
Sparse Core Ops, SparseCore 0:
  67.2 24.0 reduce-scatter.2
  94.3 31.7 reduce-scatter.4
where the time goes:
time: 133 us
  waiting for transfers between devices  58.9 us (44%)
  local copies, waits for them, and re-layouts  22.7 us (17%)
  matrix products  20.5 us (15%)
  between operations  13.5 us (10%)
  starting transfers between devices  11.2 us (8%)
  other arithmetic  5.96 us (4%)
    reduce_scatter x1, waiting for transfers between devices, shards(): lax.psum_scatter(sectioned, 'grp', scatter_dimension=0, tiled=True)  34.8 us
    reduce_scatter x1, waiting for transfers between devices, shards(): lax.psum_scatter(contributions, 'sub', scatter_dimension=0, tiled=True)  24.2 us
    ppermute x2, starting transfers between devices, extended(): lax.ppermute(lax.slice_in_dim(block, block.shape[dim] - width, None, axis...  8.63 us
    dot_general x1, matrix products, shards(): jnp.dot(margin, inverse_local, preferred_element_type=jnp.float32)  8.42 us
    reshape x4, local copies, waits for them, and re-layouts, select_panels(): panels = values.reshape(K, NB, PANEL)  7.71 us
    convert_element_type x4, other arithmetic, live_slots(): alive_mask = (jnp.arange(CMAX) < live_count).astype(values.dtype)  4.61 us
    reshape x1, local copies, waits for them, and re-layouts, shards(): rows_margin = jnp.stack(picked, axis=1).reshape(K, 4 * slot_width)  4.39 us
    dot_general x4, matrix products, select_panels(): jnp.einsum('knp,cn->kcp', panels, picker, preferred_element_type=jnp.floa...  3.59 us
  transfers between devices with their start and end apart: 6, of which 2 were waited for; matrix products, arithmetic and copies ran while one was open for 16% of the time, Pallas kernels for 0%

commit v1 on v0

v1 whole, which is shorter than its diff:
```python
import jax
import jax.numpy as jnp
from jax import lax
from jax.experimental import pallas as pl
from jax.experimental.pallas import tpu as pltpu
from jax.sharding import PartitionSpec as P

PANEL = 128
F32 = jnp.float32
BF16 = jnp.bfloat16


def swaps(count):
    even = [(i, i + 1) for i in range(0, count - 1, 2)]
    odd = [(i, i + 1) for i in range(1, count - 1, 2)]
    return [both + [(b, a) for a, b in both] for both in (even, odd)]


def split_dot(table, values, contract):
    high = values.astype(BF16)
    low = (values - high.astype(F32)).astype(BF16)
    dims = (contract, ((), ()))
    return lax.dot_general(table, high, dims, preferred_element_type=F32) + lax.dot_general(
        table, low, dims, preferred_element_type=F32
    )


def subdomain_kernel(
    scale, index_ref, count_ref, owner_ref, first_ref, even_sub, odd_sub, odd_grp, even_grp,
    coupling_ref, inverse_ref, stiffness_ref, out_ref, picked, margin,
):
    columns = even_sub.shape[0]
    slots = index_ref.shape[-1]
    grp_odd = lax.rem(lax.axis_index("grp"), 2)
    sub_odd = lax.rem(lax.axis_index("sub"), 2)
    arrivals = (
        (even_sub, 3 - sub_odd),
        (odd_sub, 2 + sub_odd),
        (odd_grp, grp_odd),
        (even_grp, 1 - grp_odd),
    )
    for number, (values, direction) in enumerate(arrivals):
        live = count_ref[0, 0, direction]
        for slot in range(slots):
            place = index_ref[0, 0, direction, slot]
            panel = values[:, pl.ds(pl.multiple_of(place * PANEL, PANEL), PANEL)]
            alive = jnp.where(slot < live, 1.0, 0.0).astype(BF16)
            picked[:, slot * PANEL : (slot + 1) * PANEL] = panel * alive
        product = jnp.dot(picked[...], coupling_ref[direction], preferred_element_type=F32)
        if number == 0:
            margin[...] = product
        else:
            margin[...] += product
    extension = (
        first_ref[...]
        + jnp.dot(margin[...].astype(BF16), inverse_ref[...], preferred_element_type=F32)
    ).astype(BF16)
    projected = jnp.dot(extension, stiffness_ref[...], preferred_element_type=F32).astype(BF16)
    last = ((1,), (1,))
    coarse = (
        lax.dot_general(projected, extension, (last, ((), ())), preferred_element_type=F32) * scale
    )
    places = lax.broadcasted_iota(jnp.int32, (out_ref.shape[0], columns), 0)
    table = (owner_ref[0] == places).astype(F32).astype(BF16)
    turned = split_dot(table, coarse, last)
    out_ref[...] = split_dot(table, turned, last).astype(out_ref.dtype)


def shards(basis, stiffness, inverse, coupling, panel_index, panel_count, owner_map):
    basis, stiffness, inverse, coupling = (a[0, 0] for a in (basis, stiffness, inverse, coupling))
    columns, rows = basis.shape
    blocks = lax.axis_size("grp") * lax.axis_size("sub")
    own = 8
    columns_all = own * blocks
    even_sub, odd_sub = swaps(lax.axis_size("sub"))
    even_grp, odd_grp = swaps(lax.axis_size("grp"))
    from_even_grp = lax.ppermute(basis, "grp", even_grp)
    from_odd_grp = lax.ppermute(basis, "grp", odd_grp)
    from_odd_sub = lax.ppermute(basis, "sub", odd_sub)
    from_even_sub = lax.ppermute(basis, "sub", even_sub)
    first = jnp.dot(basis, inverse, preferred_element_type=F32)
    vmem = pl.BlockSpec(memory_space=pltpu.VMEM)
    smem = pl.BlockSpec(memory_space=pltpu.SMEM)
    scale = float(rows * columns) ** -0.5
    flops = 2 * columns * rows * (coupling.shape[0] * coupling.shape[1] + 2 * rows + columns)
    contributions = pl.pallas_call(
        lambda *refs: subdomain_kernel(scale, *refs),
        out_shape=jax.ShapeDtypeStruct((columns_all, columns_all), BF16),
        in_specs=[smem, smem] + [vmem] * 9,
        out_specs=vmem,
        scratch_shapes=[
            pltpu.VMEM((columns, coupling.shape[1]), BF16),
            pltpu.VMEM((columns, rows), F32),
        ],
        cost_estimate=pl.CostEstimate(flops=flops, bytes_accessed=12 * 2**20, transcendentals=0),
    )(
        panel_index, panel_count, owner_map, first,
        from_even_sub, from_odd_sub, from_odd_grp, from_even_grp,
        coupling, inverse, stiffness,
    )
    parts = lax.all_to_all(
        contributions.reshape(blocks, own, columns_all), ("grp", "sub"), 0, 0, tiled=True
    )
    return jnp.sum(parts.astype(F32), axis=0)


def solution(mesh):
    three, four = P("grp", "sub", None), P("grp", "sub", None, None)
    in_specs = (four, four, four, P("grp", "sub", None, None, None), four, three, three)
    out_specs = P(("grp", "sub"), None)
    return jax.shard_map(shards, mesh=mesh, in_specs=in_specs, out_specs=out_specs, check_vma=False)
```

time: 133 us -> 50.3 us (0.38)
  waiting for transfers between devices: 58.9 us -> 7 us
  local copies, waits for them, and re-layouts: 22.7 us -> 1.05 us
  matrix products: 20.5 us -> 4.07 us
  blocking collectives: 0 us -> 15.1 us
  between operations: 13.5 us -> 0.05 us
  Pallas kernels: 0 us -> 12.6 us
  other arithmetic: 5.96 us -> 0.63 us
  starting transfers between devices: 11.2 us -> 9.54 us
    reduce_scatter x2 -> x0, waiting for transfers between devices: 58.9 us -> none  [the longest x1 34.8 us: shards(): lax.psum_scatter(sectioned, 'grp', scatter_dimension=0, tiled=True)]
    dot_general x9 -> x1, matrix products: 20.5 us -> 4.07 us  [shards(): first = jnp.dot(basis, inverse, preferred_element_type=F32)]
    all_to_all x0 -> x1, blocking collectives: none -> 15.1 us  [shards(): lax.all_to_all(contributions.reshape(blocks, own, columns_all), ('grp', '...]
    pallas_call x0 -> x1, Pallas kernels: none -> 12.6 us  [shards(): pl.pallas_call(lambda *refs: subdomain_kernel(scale, *refs), out_shape=ja...]
    reshape x5 -> x0, local copies, waits for them, and re-layouts: 12.1 us -> none  [the longest x4 7.71 us: select_panels(): panels = values.reshape(K, NB, PANEL)]
    ppermute x4, waiting for transfers between devices: 0.01 us -> 7 us  [the longest x1 7 us: shards(): from_even_sub = lax.ppermute(basis, 'sub', even_sub)]
    ppermute x4 -> x0, local copies, waits for them, and re-layouts: 5.95 us -> none  [the longest x2 2.98 us: extended(): lax.ppermute(lax.slice_in_dim(block, 0, width, axis=dim), axis, backward)]
    convert_element_type x4 -> x0, other arithmetic: 4.61 us -> none  [live_slots(): alive_mask = (jnp.arange(CMAX) < live_count).astype(values.dtype)]
  transfers between devices with their start and end apart: 6 -> 4, of which waited for: 2 -> 1; matrix products, arithmetic and copies ran while one was open for 16% -> 8% of each run, Pallas kernels for 0% -> 0%
where the time goes in v1:
time: 50.3 us; the launch traced here: 50.1 us
  blocking collectives  15.1 us (30%)
  Pallas kernels  12.6 us (25%)
  starting transfers between devices  9.54 us (19%)
  waiting for transfers between devices  7 us (14%)
  matrix products  4.07 us (8%)
  local copies, waits for them, and re-layouts  1.05 us (2%)
  other arithmetic  0.63 us (1%)
    all_to_all x1, blocking collectives, shards(): lax.all_to_all(contributions.reshape(blocks, own, columns_all), ('grp', '...  15.1 us
    pallas_call x1, Pallas kernels, shards(): pl.pallas_call(lambda *refs: subdomain_kernel(scale, *refs), out_shape=ja...  12.6 us
    ppermute x1, waiting for transfers between devices, shards(): from_even_sub = lax.ppermute(basis, 'sub', even_sub)  7 us
    ppermute x1, starting transfers between devices, shards(): from_even_sub = lax.ppermute(basis, 'sub', even_sub)  5.9 us
    dot_general x1, matrix products, shards(): first = jnp.dot(basis, inverse, preferred_element_type=F32)  4.07 us
    ppermute x1, starting transfers between devices, shards(): from_even_grp = lax.ppermute(basis, 'grp', even_grp)  2.25 us
    unnamed x8, local copies, waits for them, and re-layouts  1.05 us
  transfers between devices with their start and end apart: 4, of which 1 were waited for; matrix products, arithmetic and copies ran while one was open for 8% of the time, Pallas kernels for 0%

profile of v1, /device:TPU:0, one launch (start us, length us, event | category | flops | bytes accessed | tf_op | source)
XLA Modules:
  0.0 50.1 jit_solution(17517239144834419285)
XLA Ops:
  0.0 0.7 %collective-permute-start.2 = (bf16[270,1152]{1,0:T(8,128)(2,1)}, bf16[270,1152]{1,0:T(8,128)(2,1)S(1)}, u32[]{:S(2)}, u32[]{:S(2)}) collective-permute-start(bf16[270,1152]{1,0:T(8,128)(2,1)} %bitcast.13), channel_id=1, source_target_pairs={{4,8},{12,16},{20,24},{8,4},{16,12},{24,20},{5,9},{13,17},{21,25},... | collective-permute-start | bytes 1866248 | tf_op jit(solution)/shard_map/ppermute | solution.py:78
  0.7 0.7 %collective-permute-start.1 = (bf16[270,1152]{1,0:T(8,128)(2,1)}, bf16[270,1152]{1,0:T(8,128)(2,1)S(1)}, u32[]{:S(2)}, u32[]{:S(2)}) collective-permute-start(bf16[270,1152]{1,0:T(8,128)(2,1)} %bitcast.14), channel_id=1, source_target_pairs={{1,2},{2,1},{5,6},{6,5},{9,10},{10,9},{13,14},{14,13},{17,18},{18,... | collective-permute-start | bytes 1866248 | tf_op jit(solution)/shard_map/ppermute | solution.py:79
  1.4 5.9 %collective-permute-start = (bf16[270,1152]{1,0:T(8,128)(2,1)}, bf16[270,1152]{1,0:T(8,128)(2,1)S(1)}, u32[]{:S(2)}, u32[]{:S(2)}) collective-permute-start(bf16[270,1152]{1,0:T(8,128)(2,1)} %bitcast.15), channel_id=1, source_target_pairs={{0,1},{2,3},{1,0},{3,2},{4,5},{6,7},{5,4},{7,6},{8,9},{10,11},{9,8... | collective-permute-start | bytes 1866248 | tf_op jit(solution)/shard_map/ppermute | solution.py:80
  7.3 2.3 %collective-permute-start.3 = (bf16[270,1152]{1,0:T(8,128)(2,1)}, bf16[270,1152]{1,0:T(8,128)(2,1)S(1)}, u32[]{:S(2)}, u32[]{:S(2)}) collective-permute-start(bf16[270,1152]{1,0:T(8,128)(2,1)} %bitcast.16), channel_id=1, source_target_pairs={{0,4},{8,12},{16,20},{24,28},{4,0},{12,8},{20,16},{28,24},{1,5},{9... | collective-permute-start | bytes 1866248 | tf_op jit(solution)/shard_map/ppermute | solution.py:77
  9.6 4.1 %fusion.refs_3_ = f32[270,1152]{1,0:T(8,128)} fusion(bf16[1,1,1152,1152]{3,2,1,0:T(8,128)(2,1)} %param.9, bf16[1,1,270,1152]{3,2,1,0:T(8,128)(2,1)} %param.7), kind=kOutput, calls=%fused_computation.1 | convolution fusion | flops 716636160 | bytes 4520448 | tf_op jit(solution)/shard_map/dot_general | solution.py:81
  13.6 0.0 collective-permute-done.2.refs_6_
  13.6 0.0 copy-start
  13.6 0.0 collective-permute-done.1.refs_5_
  13.6 0.0 copy-start.1
  13.7 7.0 %collective-permute-done.refs_4_ = bf16[270,1152]{1,0:T(8,128)(2,1)S(1)} collective-permute-done((bf16[270,1152]{1,0:T(8,128)(2,1)}, bf16[270,1152]{1,0:T(8,128)(2,1)S(1)}, u32[]{:S(2)}, u32[]{:S(2)}) %collective-permute-start) | collective-permute-done | bytes 622112 | tf_op jit(solution)/shard_map/ppermute | solution.py:80
  20.6 0.0 copy-start.2
  20.6 0.0 collective-permute-done.3.refs_7_
  20.7 0.0 copy-start.3
  20.7 0.0 copy-done
  20.7 0.0 copy-done.1
  20.7 0.8 %copy-done.2 = bf16[270,1152]{1,0:T(8,128)(2,1)} copy-done((bf16[270,1152]{1,0:T(8,128)(2,1)}, bf16[270,1152]{1,0:T(8,128)(2,1)S(1)}, u32[]{:S(2)}) %copy-start.2) | copy-done | bytes 622104
  21.5 0.2 copy-done.3
  21.7 12.6 %shard_map.73 = bf16[256,256]{1,0:T(8,128)(2,1)} custom-call(s32[1,1,4,6]{3,2,1,0:T(4,128)} %refs_0_.1, s32[1,1,4]{2,1,0:T(1,128)} %refs_1_.1, s32[1,1,270]{2,1,0:T(1,128)} %refs_2_.1, f32[270,1152]{1,0:T(8,128)} %fusion.refs_3_, bf16[270,1152]{1,0:T(8,128)(2,1)} %copy-done.2, bf16[270,1152]{1,0:T(8,128)(2,1)} %copy-done.1, bf16[270,1152]{1,0:T(8,128)(2,1)} %copy-done, ...), custom_call_target="tpu_custom_call" | custom-call | flops 3512263680 | bytes 12582912 | tf_op jit(solution)/shard_map/pallas_call | solution.py:86
  34.3 15.1 %all_to_all.5 = bf16[32,8,256]{2,1,0:T(8,128)(2,1)S(1)} all-to-all(bf16[32,8,256]{2,1,0:T(8,128)(2,1)} %bitcast.12), channel_id=1, replica_groups=mesh['grp'=8,'sub'=4] {'grp','sub'}, dimensions={0} | all-to-all | bytes 262144 | tf_op jit(solution)/shard_map/all_to_all | solution.py:101
  49.5 0.6 %convert_reduce_fusion = f32[8,256]{1,0:T(8,128)} fusion(bf16[32,8,256]{2,1,0:T(8,128)(2,1)S(1)} %all_to_all.5), kind=kLoop, calls=%fused_computation | loop fusion | flops 129024 | bytes 139264 | tf_op jit(solution)/shard_map/reduce_sum | solution.py:104
Async XLA Ops:
  0.0 13.6 %collective-permute-start.2 = (bf16[270,1152]{1,0:T(8,128)(2,1)}, bf16[270,1152]{1,0:T(8,128)(2,1)S(1)}, u32[]{:S(2)}, u32[]{:S(2)}) collective-permute-start(bf16[270,1152]{1,0:T(8,128)(2,1)} %bitcast.13), channel_id=1, source_target_pairs={{4,8},{12,16},{20,24},{8,4},{16,12},{24,20},{5,9},{13,17},{21,25},... | collective-permute-start | bytes 1866248 | tf_op jit(solution)/shard_map/ppermute | solution.py:78
  0.7 12.9 %collective-permute-start.1 = (bf16[270,1152]{1,0:T(8,128)(2,1)}, bf16[270,1152]{1,0:T(8,128)(2,1)S(1)}, u32[]{:S(2)}, u32[]{:S(2)}) collective-permute-start(bf16[270,1152]{1,0:T(8,128)(2,1)} %bitcast.14), channel_id=1, source_target_pairs={{1,2},{2,1},{5,6},{6,5},{9,10},{10,9},{13,14},{14,13},{17,18},{18,... | collective-permute-start | bytes 1866248 | tf_op jit(solution)/shard_map/ppermute | solution.py:79
  1.4 19.2 %collective-permute-start = (bf16[270,1152]{1,0:T(8,128)(2,1)}, bf16[270,1152]{1,0:T(8,128)(2,1)S(1)}, u32[]{:S(2)}, u32[]{:S(2)}) collective-permute-start(bf16[270,1152]{1,0:T(8,128)(2,1)} %bitcast.15), channel_id=1, source_target_pairs={{0,1},{2,3},{1,0},{3,2},{4,5},{6,7},{5,4},{7,6},{8,9},{10,11},{9,8... | collective-permute-start | bytes 1866248 | tf_op jit(solution)/shard_map/ppermute | solution.py:80
  7.3 13.3 %collective-permute-start.3 = (bf16[270,1152]{1,0:T(8,128)(2,1)}, bf16[270,1152]{1,0:T(8,128)(2,1)S(1)}, u32[]{:S(2)}, u32[]{:S(2)}) collective-permute-start(bf16[270,1152]{1,0:T(8,128)(2,1)} %bitcast.16), channel_id=1, source_target_pairs={{0,4},{8,12},{16,20},{24,28},{4,0},{12,8},{20,16},{28,24},{1,5},{9... | collective-permute-start | bytes 1866248 | tf_op jit(solution)/shard_map/ppermute | solution.py:77
  13.6 7.0 %copy-start = (bf16[270,1152]{1,0:T(8,128)(2,1)}, bf16[270,1152]{1,0:T(8,128)(2,1)S(1)}, u32[]{:S(2)}) copy-start(bf16[270,1152]{1,0:T(8,128)(2,1)S(1)} %collective-permute-done.2.refs_6_) | copy-start | bytes 1866244
  13.6 7.0 %copy-start.1 = (bf16[270,1152]{1,0:T(8,128)(2,1)}, bf16[270,1152]{1,0:T(8,128)(2,1)S(1)}, u32[]{:S(2)}) copy-start(bf16[270,1152]{1,0:T(8,128)(2,1)S(1)} %collective-permute-done.1.refs_5_) | copy-start | bytes 1866244
  20.6 0.9 %copy-start.2 = (bf16[270,1152]{1,0:T(8,128)(2,1)}, bf16[270,1152]{1,0:T(8,128)(2,1)S(1)}, u32[]{:S(2)}) copy-start(bf16[270,1152]{1,0:T(8,128)(2,1)S(1)} %collective-permute-done.refs_4_) | copy-start | bytes 1866244
  20.7 1.1 %copy-start.3 = (bf16[270,1152]{1,0:T(8,128)(2,1)}, bf16[270,1152]{1,0:T(8,128)(2,1)S(1)}, u32[]{:S(2)}) copy-start(bf16[270,1152]{1,0:T(8,128)(2,1)S(1)} %collective-permute-done.3.refs_7_) | copy-start | bytes 1866244

commit v2 on v1

v2 whole, which is shorter than its diff:
```python
import jax
import jax.numpy as jnp
import numpy as np
from jax import lax
from jax.experimental import pallas as pl
from jax.experimental.pallas import tpu as pltpu
from jax.sharding import PartitionSpec as P

PANEL = 128
OWN = 8
F32 = jnp.float32
BF16 = jnp.bfloat16
EARLY, MIDDLE, LATE = 3, (0,), (1, 2)
ORDER = (0, 1, 2, 3)
VMEM = pl.BlockSpec(memory_space=pltpu.VMEM)
SMEM = pl.BlockSpec(memory_space=pltpu.SMEM)


def exchange_rounds(groups, members):
    rounds = [[], [], [], []]
    for g in range(groups):
        inner = g % 4 in (1, 2)
        across = g + 1 < groups if g % 2 else g > 0
        turns = ("BXA" if inner else "ABX") if across else "AB"
        for s in range(members - 1):
            rounds[turns.index("BA"[s % 2 == 0])].append(((g, s), (g, s + 1)))
        if g + 1 < groups:
            for s in range(members):
                if g % 2 == 0:
                    number = 3
                elif s == 0 or s == members - 1 and s % 2:
                    number = min({0, 1, 2} - {turns.index("A")})
                else:
                    number = turns.index("X")
                rounds[number].append(((g, s), (g + 1, s)))
    sources = np.full((groups * members, len(rounds)), -1, np.int32)
    swaps = []
    for number, pairs in enumerate(rounds):
        flat = []
        for low, high in pairs:
            a, b = (g * members + s for g, s in (low, high))
            along_sub = low[0] == high[0]
            assert max(sources[a, number], sources[b, number]) < 0
            sources[a, number] = 3 if along_sub else 1
            sources[b, number] = 2 if along_sub else 0
            flat += [(a, b), (b, a)]
        swaps.append(flat)
    return swaps, sources


def margin_product(number, me, source_ref, index_ref, count_ref, values, coupling_ref, picked):
    source = source_ref[me, number]
    direction = jnp.maximum(source, 0)
    live = count_ref[0, 0, direction]
    for slot in range(index_ref.shape[-1]):
        place = index_ref[0, 0, direction, slot]
        panel = values[:, pl.ds(pl.multiple_of(place * PANEL, PANEL), PANEL)]
        alive = jnp.where(slot < live, 1.0, 0.0).astype(BF16)
        picked[:, slot * PANEL : (slot + 1) * PANEL] = panel * alive
    return jnp.dot(picked[...], coupling_ref[direction], preferred_element_type=F32)


def place_of():
    return lax.axis_index("grp") * lax.axis_size("sub") + lax.axis_index("sub")


def early_kernel(
    number, source_ref, index_ref, count_ref, owner_ref, values, coupling_ref,
    out_ref, table_ref, turned_ref, picked,
):
    out_ref[...] = margin_product(
        number, place_of(), source_ref, index_ref, count_ref, values, coupling_ref, picked
    )
    places = lax.broadcasted_iota(jnp.int32, table_ref.shape, 0)
    table = (owner_ref[0] == places).astype(F32)
    table_ref[...] = table.astype(BF16)
    turned_ref[...] = table.T.astype(BF16)


def next_kernel(number, source_ref, index_ref, count_ref, values, coupling_ref, so_far, out_ref, picked):
    out_ref[...] = so_far[...] + margin_product(
        number, place_of(), source_ref, index_ref, count_ref, values, coupling_ref, picked
    )


def last_kernel(
    numbers, scale, source_ref, index_ref, count_ref, table_ref, turned_ref, first_ref, so_far, *refs
):
    arrived = refs[: len(numbers)]
    coupling_ref, inverse_ref, stiffness_ref, out_ref, picked, margin = refs[len(numbers) :]
    columns = margin.shape[0]
    me = place_of()
    for at, (number, values) in enumerate(zip(numbers, arrived)):
        product = margin_product(
            number, me, source_ref, index_ref, count_ref, values, coupling_ref, picked
        )
        margin[...] = (so_far if at == 0 else margin)[...] + product
    extension = (
        first_ref[...]
        + jnp.dot(margin[...].astype(BF16), inverse_ref[...], preferred_element_type=F32)
    ).astype(BF16)
    projected = jnp.dot(extension, stiffness_ref[...], preferred_element_type=F32).astype(BF16)
    coarse = lax.dot_general(
        projected, extension, (((1,), (1,)), ((), ())), preferred_element_type=F32
    )
    coarse = (coarse * scale).astype(BF16)
    placed = jnp.dot(table_ref[...], coarse, preferred_element_type=F32).astype(BF16)
    out_ref[...] = jnp.dot(placed, turned_ref[...], preferred_element_type=F32).astype(BF16)


def shards(swaps, sources, basis, stiffness, inverse, coupling, panel_index, panel_count, owner_map):
    basis, stiffness, inverse, coupling = (a[0, 0] for a in (basis, stiffness, inverse, coupling))
    columns, rows = basis.shape
    blocks = lax.axis_size("grp") * lax.axis_size("sub")
    columns_all = OWN * blocks
    arrivals = [None] * len(swaps)
    for number in ORDER:
        arrivals[number] = lax.ppermute(basis, ("grp", "sub"), swaps[number])
    first = jnp.dot(basis, inverse, preferred_element_type=F32)
    coupling, inverse, stiffness = (
        pltpu.with_memory_space_constraint(a, pltpu.VMEM) for a in (coupling, inverse, stiffness)
    )
    tables = (jnp.asarray(sources), panel_index, panel_count)
    scale = float(rows * columns) ** -0.5
    slots_wide = coupling.shape[1]
    picked = pltpu.VMEM((columns, slots_wide), BF16)
    step = 2 * columns * slots_wide * rows
    room = 8 * 2**20 + 4 * columns_all**2
    params = pltpu.CompilerParams(vmem_limit_bytes=room)
    margin, table, turned = pl.pallas_call(
        lambda *refs: early_kernel(EARLY, *refs),
        out_shape=(
            jax.ShapeDtypeStruct((columns, rows), F32),
            jax.ShapeDtypeStruct((columns_all, columns), BF16),
            jax.ShapeDtypeStruct((columns, columns_all), BF16),
        ),
        in_specs=[SMEM] * 3 + [VMEM] * 3,
        out_specs=(VMEM,) * 3,
        scratch_shapes=[picked],
        cost_estimate=pl.CostEstimate(flops=step, bytes_accessed=3 * 2**20, transcendentals=0),
        compiler_params=params,
    )(*tables, owner_map, arrivals[EARLY], coupling)
    for number in MIDDLE:
        margin = pl.pallas_call(
            lambda *refs, number=number: next_kernel(number, *refs),
            out_shape=jax.ShapeDtypeStruct((columns, rows), F32),
            in_specs=[SMEM] * 3 + [VMEM] * 3,
            out_specs=VMEM,
            scratch_shapes=[picked],
            cost_estimate=pl.CostEstimate(flops=step, bytes_accessed=3 * 2**20, transcendentals=0),
            compiler_params=params,
        )(*tables, arrivals[number], coupling, margin)
    contributions = pl.pallas_call(
        lambda *refs: last_kernel(LATE, scale, *refs),
        out_shape=jax.ShapeDtypeStruct((columns_all, columns_all), BF16),
        in_specs=[SMEM] * 3 + [VMEM] * (7 + len(LATE)),
        out_specs=VMEM,
        scratch_shapes=[picked, pltpu.VMEM((columns, rows), F32)],
        cost_estimate=pl.CostEstimate(
            flops=step * len(LATE) + 2 * columns * rows * (2 * rows + columns),
            bytes_accessed=12 * 2**20,
            transcendentals=0,
        ),
        compiler_params=params,
    )(*tables, table, turned, first, margin, *(arrivals[n] for n in LATE), coupling, inverse, stiffness)
    parts = lax.all_to_all(
        contributions.reshape(blocks, OWN, columns_all), ("grp", "sub"), 0, 0, tiled=True
    )
    return jnp.sum(parts.astype(F32), axis=0)


def solution(mesh):
    three, four = P("grp", "sub", None), P("grp", "sub", None, None)
    in_specs = (four, four, four, P("grp", "sub", None, None, None), four, three, three)
    out_specs = P(("grp", "sub"), None)
    swaps, sources = exchange_rounds(mesh.shape["grp"], mesh.shape["sub"])
    return jax.shard_map(
        lambda *args: shards(swaps, sources, *args),
        mesh=mesh, in_specs=in_specs, out_specs=out_specs, check_vma=False,
    )
```

time: 50.3 us -> 39.3 us (0.78)
  waiting for transfers between devices: 7 us -> 0.01 us
  starting transfers between devices: 9.54 us -> 4.6 us
  local copies, waits for them, and re-layouts: 1.05 us -> 5.33 us
  Pallas kernels: 12.6 us -> 8.42 us
  blocking collectives: 15.1 us -> 16.9 us
  matrix products: 4.07 us -> 3.01 us
    ppermute x4, waiting for transfers between devices: 7 us -> 0.01 us  [shards(): arrivals[number] = lax.ppermute(basis, ('grp', 'sub'), swaps[number])]
    ppermute x4, starting transfers between devices: 9.54 us -> 4.6 us  [shards(): arrivals[number] = lax.ppermute(basis, ('grp', 'sub'), swaps[number])]
    unnamed x8 -> x16, local copies, waits for them, and re-layouts: 1.05 us -> 5.33 us
    pallas_call x1 -> x3, Pallas kernels: 12.6 us -> 8.42 us  [the longest x1 5.21 us: shards(): pl.pallas_call(lambda *refs: last_kernel(LATE, scale, *refs), out_shape=j...]
    all_to_all x1, blocking collectives: 15.1 us -> 16.9 us  [shards(): lax.all_to_all(contributions.reshape(blocks, OWN, columns_all), ('grp', '...]
    dot_general x1, matrix products: 4.07 us -> 3.01 us  [shards(): first = jnp.dot(basis, inverse, preferred_element_type=F32)]
  transfers between devices with their start and end apart: 4 -> 4, of which waited for: 1 -> 0; matrix products, arithmetic and copies ran while one was open for 8% -> 8% of each run, Pallas kernels for 0% -> 8%
where the time goes in v2:
time: 39.3 us; the launch traced here: 39 us
  blocking collectives  16.9 us (43%)
  Pallas kernels  8.42 us (21%)
  local copies, waits for them, and re-layouts  5.33 us (14%)
  starting transfers between devices  4.6 us (12%)
  matrix products  3.01 us (8%)
  other arithmetic  0.63 us (2%)
    all_to_all x1, blocking collectives, shards(): lax.all_to_all(contributions.reshape(blocks, OWN, columns_all), ('grp', '...  16.9 us
    unnamed x16, local copies, waits for them, and re-layouts  5.33 us
    pallas_call x1, Pallas kernels, shards(): pl.pallas_call(lambda *refs: last_kernel(LATE, scale, *refs), out_shape=j...  5.21 us
    ppermute x4, starting transfers between devices, shards(): arrivals[number] = lax.ppermute(basis, ('grp', 'sub'), swaps[number])  4.6 us
    dot_general x1, matrix products, shards(): first = jnp.dot(basis, inverse, preferred_element_type=F32)  3.01 us
    pallas_call x1, Pallas kernels, shards(): pl.pallas_call(lambda *refs, number=number: next_kernel(number, *refs), o...  1.62 us
    pallas_call x1, Pallas kernels, shards(): pl.pallas_call(lambda *refs: early_kernel(EARLY, *refs), out_shape=(jax.S...  1.58 us
  transfers between devices with their start and end apart: 4, of which 0 were waited for; matrix products, arithmetic and copies ran while one was open for 8% of the time, Pallas kernels for 8%

profile of v2, /device:TPU:0, one launch (start us, length us, event | category | flops | bytes accessed | tf_op | source)
XLA Modules:
  0.0 39.0 jit_solution(8935062262158701312)
XLA Ops:
  0.0 0.0 copy-start.4
  0.0 0.6 %collective-permute-start = (bf16[270,1152]{1,0:T(8,128)(2,1)}, bf16[270,1152]{1,0:T(8,128)(2,1)S(1)}, u32[]{:S(2)}, u32[]{:S(2)}) collective-permute-start(bf16[270,1152]{1,0:T(8,128)(2,1)} %bitcast.15), channel_id=1, source_target_pairs={{0,4},{4,0},{1,5},{5,1},{2,6},{6,2},{3,7},{7,3},{8,12},{12,8},{9,1... | collective-permute-start | bytes 1866248 | tf_op jit(solution)/shard_map/ppermute | solution.py:118
  0.6 2.6 %collective-permute-start.1 = (bf16[270,1152]{1,0:T(8,128)(2,1)}, bf16[270,1152]{1,0:T(8,128)(2,1)S(1)}, u32[]{:S(2)}, u32[]{:S(2)}) collective-permute-start(bf16[270,1152]{1,0:T(8,128)(2,1)} %bitcast.16), channel_id=1, source_target_pairs={{0,1},{1,0},{2,3},{3,2},{5,6},{6,5},{4,8},{8,4},{7,11},{11,7},{9,1... | collective-permute-start | bytes 1866248 | tf_op jit(solution)/shard_map/ppermute | solution.py:118
  3.2 0.7 %collective-permute-start.2 = (bf16[270,1152]{1,0:T(8,128)(2,1)}, bf16[270,1152]{1,0:T(8,128)(2,1)S(1)}, u32[]{:S(2)}, u32[]{:S(2)}) collective-permute-start(bf16[270,1152]{1,0:T(8,128)(2,1)} %bitcast.17), channel_id=1, source_target_pairs={{1,2},{2,1},{5,9},{9,5},{6,10},{10,6},{13,14},{14,13},{12,16},{16,... | collective-permute-start | bytes 1866248 | tf_op jit(solution)/shard_map/ppermute | solution.py:118
  3.9 0.7 %collective-permute-start.3 = (bf16[270,1152]{1,0:T(8,128)(2,1)}, bf16[270,1152]{1,0:T(8,128)(2,1)S(1)}, u32[]{:S(2)}, u32[]{:S(2)}) collective-permute-start(bf16[270,1152]{1,0:T(8,128)(2,1)} %bitcast.18), channel_id=1, source_target_pairs={{4,5},{5,4},{6,7},{7,6},{8,9},{9,8},{10,11},{11,10},{13,17},{17,13... | collective-permute-start | bytes 1866248 | tf_op jit(solution)/shard_map/ppermute | solution.py:118
  4.6 3.0 %fusion.refs_5_ = f32[270,1152]{1,0:T(8,128)S(1)} fusion(bf16[1,1,1152,1152]{3,2,1,0:T(8,128)(2,1)} %param.10, bf16[1,1,270,1152]{3,2,1,0:T(8,128)(2,1)} %param.8), kind=kOutput, calls=%fused_computation.1 | convolution fusion | flops 716636160 | bytes 4520448 | tf_op jit(solution)/shard_map/dot_general | solution.py:119
  7.6 0.0 collective-permute-done.refs_4_
  7.7 0.0 copy-done.4
  7.7 0.0 copy-done.5
  7.7 0.0 copy-done.6
  7.7 0.0 copy-done.7
  7.7 0.0 copy-start
  7.7 3.0 %copy-done = bf16[1,1,4,768,1152]{4,3,2,1,0:T(8,128)(2,1)S(1)} copy-done((bf16[1,1,4,768,1152]{4,3,2,1,0:T(8,128)(2,1)S(1)}, bf16[1,1,4,768,1152]{4,3,2,1,0:T(8,128)(2,1)}, u32[]{:S(2)}) %copy-start) | copy-done | bytes 7077912
  10.7 1.6 %shard_map.82 = (f32[270,1152]{1,0:T(8,128)S(1)}, bf16[256,270]{1,0:T(8,128)(2,1)S(1)}, bf16[270,256]{1,0:T(8,128)(2,1)S(1)}) custom-call(s32[32,4]{1,0:T(8,128)S(1)} %copy-done.4, s32[1,1,4,6]{3,2,1,0:T(4,128)S(1)} %copy-done.5, s32[1,1,4]{2,1,0:T(1,128)S(1)} %copy-done.6, s32[1,1,270]{2,1,0:T(1,128)S(1)} %copy-done.7, ...), custom_call_target="tpu_custom_call" | custom-call | flops 477757440 | bytes 3145728 | tf_op jit(solution)/shard_map/pallas_call | solution.py:130
  12.3 0.0 collective-permute-done.1.refs_3_
  12.3 1.4 %copy-done.1 = bf16[1,1,4,768,1152]{4,3,2,1,0:T(8,128)(2,1)S(1)} copy-done((bf16[1,1,4,768,1152]{4,3,2,1,0:T(8,128)(2,1)S(1)}, bf16[1,1,4,768,1152]{4,3,2,1,0:T(8,128)(2,1)}, u32[]{:S(2)}) %copy-start.1) | copy-done | bytes 7077912
  13.7 1.6 %shard_map.83.refs_6_ = f32[270,1152]{1,0:T(8,128)S(1)} custom-call(s32[32,4]{1,0:T(8,128)S(1)} %copy-done.4, s32[1,1,4,6]{3,2,1,0:T(4,128)S(1)} %copy-done.5, s32[1,1,4]{2,1,0:T(1,128)S(1)} %copy-done.6, bf16[270,1152]{1,0:T(8,128)(2,1)S(1)} %collective-permute-done.1.refs_3_, bf16[4,768,1152]{2,1,0:T(8,128)(2,1)S(1)} %bitcast.10, ...), custom_call_target="tpu_custom_call" | custom-call | flops 477757440 | bytes 3145728 | tf_op jit(solution)/shard_map/pallas_call | solution.py:144
  15.3 0.0 collective-permute-done.2.refs_7_
  15.4 0.0 collective-permute-done.3.refs_8_
  15.4 0.1 copy-done.2
  15.5 0.8 %copy-done.3 = bf16[1,1,1152,1152]{3,2,1,0:T(8,128)(2,1)S(1)} copy-done((bf16[1,1,1152,1152]{3,2,1,0:T(8,128)(2,1)S(1)}, bf16[1,1,1152,1152]{3,2,1,0:T(8,128)(2,1)}, u32[]{:S(2)}) %copy-start.3) | copy-done | bytes 2654232
  16.3 5.2 %shard_map.84 = bf16[256,256]{1,0:T(8,128)(2,1)S(1)} custom-call(s32[32,4]{1,0:T(8,128)S(1)} %copy-done.4, s32[1,1,4,6]{3,2,1,0:T(4,128)S(1)} %copy-done.5, s32[1,1,4]{2,1,0:T(1,128)S(1)} %copy-done.6, bf16[256,270]{1,0:T(8,128)(2,1)S(1)} %get-tuple-element.8.refs_3_, bf16[270,256]{1,0:T(8,128)(2,1)S(1)} %get-tuple-element.9.refs_4_, ...), custom_call_target="tpu_custom_call" | custom-call | flops 2556748800 | bytes 12582912 | tf_op jit(solution)/shard_map/pallas_call | solution.py:153
  21.5 16.9 %all_to_all.5 = bf16[32,8,256]{2,1,0:T(8,128)(2,1)S(1)} all-to-all(bf16[32,8,256]{2,1,0:T(8,128)(2,1)S(1)} %bitcast.14), channel_id=1, replica_groups=mesh['grp'=8,'sub'=4] {'grp','sub'}, dimensions={0} | all-to-all | bytes 262144 | tf_op jit(solution)/shard_map/all_to_all | solution.py:166
  38.4 0.6 %convert_reduce_fusion = f32[8,256]{1,0:T(8,128)} fusion(bf16[32,8,256]{2,1,0:T(8,128)(2,1)S(1)} %all_to_all.5), kind=kLoop, calls=%fused_computation | loop fusion | flops 129024 | bytes 139264 | tf_op jit(solution)/shard_map/reduce_sum | solution.py:169
  (6 shorter events, 0.0 us)
Async XLA Ops:
  0.0 7.7 %copy-start.4 = (s32[32,4]{1,0:T(8,128)S(1)}, s32[32,4]{1,0:T(8,128)}, u32[]{:S(2)}) copy-start(s32[32,4]{1,0:T(8,128)} %constant.4.clone.refs_0_) | copy-start | bytes 1540
  0.0 7.7 %copy-start.5 = (s32[1,1,4,6]{3,2,1,0:T(4,128)S(1)}, s32[1,1,4,6]{3,2,1,0:T(4,128)}, u32[]{:S(2)}) copy-start(s32[1,1,4,6]{3,2,1,0:T(4,128)} %refs_1_.5) | copy-start | bytes 292
  0.0 7.7 %copy-start.6 = (s32[1,1,4]{2,1,0:T(1,128)S(1)}, s32[1,1,4]{2,1,0:T(1,128)}, u32[]{:S(2)}) copy-start(s32[1,1,4]{2,1,0:T(1,128)} %refs_2_.5) | copy-start | bytes 52
  0.0 7.7 %copy-start.7 = (s32[1,1,270]{2,1,0:T(1,128)S(1)}, s32[1,1,270]{2,1,0:T(1,128)}, u32[]{:S(2)}) copy-start(s32[1,1,270]{2,1,0:T(1,128)} %refs_3_.1) | copy-start | bytes 3244
  0.0 7.6 %collective-permute-start = (bf16[270,1152]{1,0:T(8,128)(2,1)}, bf16[270,1152]{1,0:T(8,128)(2,1)S(1)}, u32[]{:S(2)}, u32[]{:S(2)}) collective-permute-start(bf16[270,1152]{1,0:T(8,128)(2,1)} %bitcast.15), channel_id=1, source_target_pairs={{0,4},{4,0},{1,5},{5,1},{2,6},{6,2},{3,7},{7,3},{8,12},{12,8},{9,1... | collective-permute-start | bytes 1866248 | tf_op jit(solution)/shard_map/ppermute | solution.py:118
  0.6 11.7 %collective-permute-start.1 = (bf16[270,1152]{1,0:T(8,128)(2,1)}, bf16[270,1152]{1,0:T(8,128)(2,1)S(1)}, u32[]{:S(2)}, u32[]{:S(2)}) collective-permute-start(bf16[270,1152]{1,0:T(8,128)(2,1)} %bitcast.16), channel_id=1, source_target_pairs={{0,1},{1,0},{2,3},{3,2},{5,6},{6,5},{4,8},{8,4},{7,11},{11,7},{9,1... | collective-permute-start | bytes 1866248 | tf_op jit(solution)/shard_map/ppermute | solution.py:118
  3.2 12.1 %collective-permute-start.2 = (bf16[270,1152]{1,0:T(8,128)(2,1)}, bf16[270,1152]{1,0:T(8,128)(2,1)S(1)}, u32[]{:S(2)}, u32[]{:S(2)}) collective-permute-start(bf16[270,1152]{1,0:T(8,128)(2,1)} %bitcast.17), channel_id=1, source_target_pairs={{1,2},{2,1},{5,9},{9,5},{6,10},{10,6},{13,14},{14,13},{12,16},{16,... | collective-permute-start | bytes 1866248 | tf_op jit(solution)/shard_map/ppermute | solution.py:118
  3.9 11.4 %collective-permute-start.3 = (bf16[270,1152]{1,0:T(8,128)(2,1)}, bf16[270,1152]{1,0:T(8,128)(2,1)S(1)}, u32[]{:S(2)}, u32[]{:S(2)}) collective-permute-start(bf16[270,1152]{1,0:T(8,128)(2,1)} %bitcast.18), channel_id=1, source_target_pairs={{4,5},{5,4},{6,7},{7,6},{8,9},{9,8},{10,11},{11,10},{13,17},{17,13... | collective-permute-start | bytes 1866248 | tf_op jit(solution)/shard_map/ppermute | solution.py:118
  7.7 3.0 %copy-start = (bf16[1,1,4,768,1152]{4,3,2,1,0:T(8,128)(2,1)S(1)}, bf16[1,1,4,768,1152]{4,3,2,1,0:T(8,128)(2,1)}, u32[]{:S(2)}) copy-start(bf16[1,1,4,768,1152]{4,3,2,1,0:T(8,128)(2,1)} %param.11) | copy-start | bytes 21233668
  10.7 3.0 %copy-start.1 = (bf16[1,1,4,768,1152]{4,3,2,1,0:T(8,128)(2,1)S(1)}, bf16[1,1,4,768,1152]{4,3,2,1,0:T(8,128)(2,1)}, u32[]{:S(2)}) copy-start(bf16[1,1,4,768,1152]{4,3,2,1,0:T(8,128)(2,1)} %param.11) | copy-start | bytes 21233668
  13.7 1.7 %copy-start.2 = (bf16[1,1,1152,1152]{3,2,1,0:T(8,128)(2,1)S(1)}, bf16[1,1,1152,1152]{3,2,1,0:T(8,128)(2,1)}, u32[]{:S(2)}) copy-start(bf16[1,1,1152,1152]{3,2,1,0:T(8,128)(2,1)} %param.10) | copy-start | bytes 7962628
  13.7 2.5 %copy-start.3 = (bf16[1,1,1152,1152]{3,2,1,0:T(8,128)(2,1)S(1)}, bf16[1,1,1152,1152]{3,2,1,0:T(8,128)(2,1)}, u32[]{:S(2)}) copy-start(bf16[1,1,1152,1152]{3,2,1,0:T(8,128)(2,1)} %param.9) | copy-start | bytes 7962628

commit v3 on v2

--- a/solution.py
+++ b/solution.py
@@ -10,10 +10,11 @@
 OWN = 8
 F32 = jnp.float32
 BF16 = jnp.bfloat16
-EARLY, MIDDLE, LATE = 3, (0,), (1, 2)
+MIDDLE, LATE = (3, 0, 1), (2,)
 ORDER = (0, 1, 2, 3)
 VMEM = pl.BlockSpec(memory_space=pltpu.VMEM)
 SMEM = pl.BlockSpec(memory_space=pltpu.SMEM)
+HBM = pl.BlockSpec(memory_space=pltpu.HBM)
 
 
 def exchange_rounds(groups, members):
@@ -65,22 +66,40 @@
 
 
 def early_kernel(
-    number, source_ref, index_ref, count_ref, owner_ref, values, coupling_ref,
-    out_ref, table_ref, turned_ref, picked,
+    owner_ref, basis_hbm, inverse_hbm, coupling_hbm, stiffness_hbm,
+    first_ref, table_ref, turned_ref, inverse_ref, coupling_ref, stiffness_ref,
+    basis_ref, arrived,
 ):
-    out_ref[...] = margin_product(
-        number, place_of(), source_ref, index_ref, count_ref, values, coupling_ref, picked
-    )
+    copies = [
+        pltpu.make_async_copy(source, target, arrived.at[at])
+        for at, (source, target) in enumerate(
+            (
+                (basis_hbm, basis_ref),
+                (inverse_hbm, inverse_ref),
+                (coupling_hbm, coupling_ref),
+                (stiffness_hbm, stiffness_ref),
+            )
+        )
+    ]
+    for copy in copies:
+        copy.start()
     places = lax.broadcasted_iota(jnp.int32, table_ref.shape, 0)
     table = (owner_ref[0] == places).astype(F32)
     table_ref[...] = table.astype(BF16)
     turned_ref[...] = table.T.astype(BF16)
-
-
-def next_kernel(number, source_ref, index_ref, count_ref, values, coupling_ref, so_far, out_ref, picked):
-    out_ref[...] = so_far[...] + margin_product(
+    copies[0].wait()
+    copies[1].wait()
+    first_ref[...] = jnp.dot(basis_ref[...], inverse_ref[...], preferred_element_type=F32)
+    copies[2].wait()
+    copies[3].wait()
+
+
+def margin_kernel(number, source_ref, index_ref, count_ref, values, coupling_ref, *refs):
+    *so_far, out_ref, picked = refs
+    product = margin_product(
         number, place_of(), source_ref, index_ref, count_ref, values, coupling_ref, picked
     )
+    out_ref[...] = so_far[0][...] + product if so_far else product
 
 
 def last_kernel(
@@ -116,40 +135,48 @@
     arrivals = [None] * len(swaps)
     for number in ORDER:
         arrivals[number] = lax.ppermute(basis, ("grp", "sub"), swaps[number])
-    first = jnp.dot(basis, inverse, preferred_element_type=F32)
-    coupling, inverse, stiffness = (
-        pltpu.with_memory_space_constraint(a, pltpu.VMEM) for a in (coupling, inverse, stiffness)
-    )
-    tables = (jnp.asarray(sources), panel_index, panel_count)
+    stay = lambda *arrays: tuple(pltpu.with_memory_space_constraint(a, pltpu.HBM) for a in arrays)
+    tables = stay(jnp.asarray(sources), panel_index, panel_count)
     scale = float(rows * columns) ** -0.5
     slots_wide = coupling.shape[1]
     picked = pltpu.VMEM((columns, slots_wide), BF16)
     step = 2 * columns * slots_wide * rows
     room = 8 * 2**20 + 4 * columns_all**2
     params = pltpu.CompilerParams(vmem_limit_bytes=room)
-    margin, table, turned = pl.pallas_call(
-        lambda *refs: early_kernel(EARLY, *refs),
+    whole = jax.ShapeDtypeStruct((columns, rows), F32)
+    first, table, turned, inverse, coupling, stiffness = pl.pallas_call(
+        early_kernel,
         out_shape=(
-            jax.ShapeDtypeStruct((columns, rows), F32),
+            whole,
             jax.ShapeDtypeStruct((columns_all, columns), BF16),
             jax.ShapeDtypeStruct((columns, columns_all), BF16),
+            *(jax.ShapeDtypeStruct(a.shape, BF16) for a in (inverse, coupling, stiffness)),
         ),
-        in_specs=[SMEM] * 3 + [VMEM] * 3,
-        out_specs=(VMEM,) * 3,
-        scratch_shapes=[picked],
-        cost_estimate=pl.CostEstimate(flops=step, bytes_accessed=3 * 2**20, transcendentals=0),
-        compiler_params=params,
-    )(*tables, owner_map, arrivals[EARLY], coupling)
+        in_specs=[VMEM] + [HBM] * 4,
+        out_specs=(VMEM,) * 6,
+        scratch_shapes=[
+            pltpu.VMEM((columns, rows), BF16), pltpu.SemaphoreType.DMA((4,))
+        ],
+        cost_estimate=pl.CostEstimate(
+            flops=2 * columns * rows * rows, bytes_accessed=26 * 2**20, transcendentals=0
+        ),
+        compiler_params=pltpu.CompilerParams(vmem_limit_bytes=room + 16 * 2**20),
+    )(*stay(owner_map, basis, inverse, coupling, stiffness))
+    margin = ()
     for number in MIDDLE:
-        margin = pl.pallas_call(
-            lambda *refs, number=number: next_kernel(number, *refs),
-            out_shape=jax.ShapeDtypeStruct((columns, rows), F32),
-            in_specs=[SMEM] * 3 + [VMEM] * 3,
-            out_specs=VMEM,
-            scratch_shapes=[picked],
-            cost_estimate=pl.CostEstimate(flops=step, bytes_accessed=3 * 2**20, transcendentals=0),
-            compiler_params=params,
-        )(*tables, arrivals[number], coupling, margin)
+        margin = (
+            pl.pallas_call(
+                lambda *refs, number=number: margin_kernel(number, *refs),
+                out_shape=whole,
+                in_specs=[SMEM] * 3 + [VMEM] * (2 + len(margin)),
+                out_specs=VMEM,
+                scratch_shapes=[picked],
+                cost_estimate=pl.CostEstimate(
+                    flops=step, bytes_accessed=3 * 2**20, transcendentals=0
+                ),
+                compiler_params=params,
+            )(*tables, arrivals[number], coupling, *margin),
+        )
     contributions = pl.pallas_call(
         lambda *refs: last_kernel(LATE, scale, *refs),
         out_shape=jax.ShapeDtypeStruct((columns_all, columns_all), BF16),
@@ -162,7 +189,7 @@
             transcendentals=0,
         ),
         compiler_params=params,
-    )(*tables, table, turned, first, margin, *(arrivals[n] for n in LATE), coupling, inverse, stiffness)
+    )(*tables, table, turned, first, *margin, *(arrivals[n] for n in LATE), coupling, inverse, stiffness)
     parts = lax.all_to_all(
         contributions.reshape(blocks, OWN, columns_all), ("grp", "sub"), 0, 0, tiled=True
     )

time: 39.3 us -> 39.1 us (level)
  Pallas kernels: 8.42 us -> 15.2 us
  local copies, waits for them, and re-layouts: 5.33 us -> 0 us
  matrix products: 3.01 us -> 0 us
  blocking collectives: 16.9 us -> 18.2 us
    pallas_call x2 -> x4, Pallas kernels: 3.21 us -> 10.7 us  [the longest x1 5.54 us: shards(): pl.pallas_call(early_kernel, out_shape=(whole, jax.ShapeDtypeStruct((colu...]
    unnamed x16 -> x0, local copies, waits for them, and re-layouts: 5.33 us -> none
    dot_general x1 -> x0, matrix products: 3.01 us -> none  [shards(): first = jnp.dot(basis, inverse, preferred_element_type=F32)]
    all_to_all x1, blocking collectives: 16.9 us -> 18.2 us  [shards(): lax.all_to_all(contributions.reshape(blocks, OWN, columns_all), ('grp', '...]
    pallas_call x1, Pallas kernels: 5.21 us -> 4.44 us  [shards(): pl.pallas_call(lambda *refs: last_kernel(LATE, scale, *refs), out_shape=j...]
  transfers between devices with their start and end apart: 4 -> 4, of which waited for: 0 -> 1; matrix products, arithmetic and copies ran while one was open for 8% -> 0% of each run, Pallas kernels for 8% -> 28%
where the time goes in v3:
time: 39.1 us; the launch traced here: 38.7 us
  blocking collectives  18.2 us (47%)
  Pallas kernels  15.2 us (39%)
  starting transfers between devices  4.44 us (11%)
  other arithmetic  0.63 us (2%)
    all_to_all x1, blocking collectives, shards(): lax.all_to_all(contributions.reshape(blocks, OWN, columns_all), ('grp', '...  18.2 us
    pallas_call x1, Pallas kernels, shards(): pl.pallas_call(early_kernel, out_shape=(whole, jax.ShapeDtypeStruct((colu...  5.54 us
    pallas_call x3, Pallas kernels, shards(): pl.pallas_call(lambda *refs, number=number: margin_kernel(number, *refs),...  5.18 us
    ppermute x4, starting transfers between devices, shards(): arrivals[number] = lax.ppermute(basis, ('grp', 'sub'), swaps[number])  4.44 us
    pallas_call x1, Pallas kernels, shards(): pl.pallas_call(lambda *refs: last_kernel(LATE, scale, *refs), out_shape=j...  4.44 us
  transfers between devices with their start and end apart: 4, of which 1 were waited for; matrix products, arithmetic and copies ran while one was open for 0% of the time, Pallas kernels for 28%

profile of v3, /device:TPU:0, one launch (start us, length us, event | category | flops | bytes accessed | tf_op | source)
XLA Modules:
  0.0 38.7 jit_solution(3510757191102231866)
XLA Ops:
  0.0 0.5 %collective-permute-start.2 = (bf16[270,1152]{1,0:T(8,128)(2,1)}, bf16[270,1152]{1,0:T(8,128)(2,1)S(1)}, u32[]{:S(2)}, u32[]{:S(2)}) collective-permute-start(bf16[270,1152]{1,0:T(8,128)(2,1)} %bitcast.9), channel_id=1, source_target_pairs={{0,4},{4,0},{1,5},{5,1},{2,6},{6,2},{3,7},{7,3},{8,12},{12,8},{9,1... | collective-permute-start | bytes 1866248 | tf_op jit(solution)/shard_map/ppermute | solution.py:137
  0.5 2.6 %collective-permute-start.1 = (bf16[270,1152]{1,0:T(8,128)(2,1)}, bf16[270,1152]{1,0:T(8,128)(2,1)S(1)}, u32[]{:S(2)}, u32[]{:S(2)}) collective-permute-start(bf16[270,1152]{1,0:T(8,128)(2,1)} %bitcast.10), channel_id=1, source_target_pairs={{0,1},{1,0},{2,3},{3,2},{5,6},{6,5},{4,8},{8,4},{7,11},{11,7},{9,1... | collective-permute-start | bytes 1866248 | tf_op jit(solution)/shard_map/ppermute | solution.py:137
  3.1 0.7 %collective-permute-start = (bf16[270,1152]{1,0:T(8,128)(2,1)}, bf16[270,1152]{1,0:T(8,128)(2,1)S(1)}, u32[]{:S(2)}, u32[]{:S(2)}) collective-permute-start(bf16[270,1152]{1,0:T(8,128)(2,1)} %bitcast.11), channel_id=1, source_target_pairs={{1,2},{2,1},{5,9},{9,5},{6,10},{10,6},{13,14},{14,13},{12,16},{16,... | collective-permute-start | bytes 1866248 | tf_op jit(solution)/shard_map/ppermute | solution.py:137
  3.8 0.7 %collective-permute-start.3 = (bf16[270,1152]{1,0:T(8,128)(2,1)}, bf16[270,1152]{1,0:T(8,128)(2,1)S(1)}, u32[]{:S(2)}, u32[]{:S(2)}) collective-permute-start(bf16[270,1152]{1,0:T(8,128)(2,1)} %bitcast.12), channel_id=1, source_target_pairs={{4,5},{5,4},{6,7},{7,6},{8,9},{9,8},{10,11},{11,10},{13,17},{17,13... | collective-permute-start | bytes 1866248 | tf_op jit(solution)/shard_map/ppermute | solution.py:137
  4.5 5.5 %shard_map.82 = (f32[270,1152]{1,0:T(8,128)S(1)}, bf16[256,270]{1,0:T(8,128)(2,1)S(1)}, bf16[270,256]{1,0:T(8,128)(2,1)S(1)}, bf16[1152,1152]{1,0:T(8,128)(2,1)S...) custom-call(s32[1,1,270]{2,1,0:T(1,128)} %owner_ref.1, bf16[270,1152]{1,0:T(8,128)(2,1)} %bitcast.13, ...), custom_call_target="tpu_custom_call" | custom-call | flops 716636160 | bytes 27262976 | tf_op jit(solution)/shard_map/pallas_call | solution.py:147
  10.0 0.0 collective-permute-done.2.refs_3_
  10.0 1.7 %shard_map.83.refs_5_ = f32[270,1152]{1,0:T(8,128)S(1)} custom-call(s32[32,4]{1,0:T(8,128)} %constant.4.clone.refs_0_, s32[1,1,4,6]{3,2,1,0:T(4,128)} %refs_1_.7, s32[1,1,4]{2,1,0:T(1,128)} %refs_2_.7, bf16[270,1152]{1,0:T(8,128)(2,1)S(1)} %collective-permute-done.2.refs_3_, bf16[4,768,1152]{2,1,0:T(8,128)(2,1)S(1)} %get-tuple-element.14.refs_4_.refs_8_), custom_call_target="tpu_custom_call" | custom-call | flops 477757440 | bytes 3145728 | tf_op jit(solution)/shard_map/pallas_call | solution.py:168
  11.7 0.2 collective-permute-done.1.refs_3_
  11.9 1.7 %shard_map.84.refs_5_ = f32[270,1152]{1,0:T(8,128)S(1)} custom-call(s32[32,4]{1,0:T(8,128)} %constant.4.clone.refs_0_, s32[1,1,4,6]{3,2,1,0:T(4,128)} %refs_1_.7, s32[1,1,4]{2,1,0:T(1,128)} %refs_2_.7, bf16[270,1152]{1,0:T(8,128)(2,1)S(1)} %collective-permute-done.1.refs_3_, bf16[4,768,1152]{2,1,0:T(8,128)(2,1)S(1)} %get-tuple-element.14.refs_4_.refs_8_, ...), custom_call_target="tpu_custom_call" | custom-call | flops 477757440 | bytes 3145728 | tf_op jit(solution)/shard_map/pallas_call | solution.py:168
  13.7 0.0 collective-permute-done.refs_3_
  13.7 1.7 %shard_map.85.refs_6_ = f32[270,1152]{1,0:T(8,128)S(1)} custom-call(s32[32,4]{1,0:T(8,128)} %constant.4.clone.refs_0_, s32[1,1,4,6]{3,2,1,0:T(4,128)} %refs_1_.7, s32[1,1,4]{2,1,0:T(1,128)} %refs_2_.7, bf16[270,1152]{1,0:T(8,128)(2,1)S(1)} %collective-permute-done.refs_3_, bf16[4,768,1152]{2,1,0:T(8,128)(2,1)S(1)} %get-tuple-element.14.refs_4_.refs_8_, ...), custom_call_target="tpu_custom_call" | custom-call | flops 477757440 | bytes 3145728 | tf_op jit(solution)/shard_map/pallas_call | solution.py:168
  15.4 0.0 collective-permute-done.3.refs_7_
  15.4 4.4 %shard_map.86 = bf16[256,256]{1,0:T(8,128)(2,1)S(1)} custom-call(s32[32,4]{1,0:T(8,128)} %constant.4.clone.refs_0_, s32[1,1,4,6]{3,2,1,0:T(4,128)} %refs_1_.7, s32[1,1,4]{2,1,0:T(1,128)} %refs_2_.7, bf16[256,270]{1,0:T(8,128)(2,1)S(1)} %get-tuple-element.11.refs_3_, bf16[270,256]{1,0:T(8,128)(2,1)S(1)} %get-tuple-element.12.refs_4_, ...), custom_call_target="tpu_custom_call" | custom-call | flops 2078991360 | bytes 12582912 | tf_op jit(solution)/shard_map/pallas_call | solution.py:180
  19.9 18.2 %all_to_all.5 = bf16[32,8,256]{2,1,0:T(8,128)(2,1)S(1)} all-to-all(bf16[32,8,256]{2,1,0:T(8,128)(2,1)S(1)} %bitcast.5), channel_id=1, replica_groups=mesh['grp'=8,'sub'=4] {'grp','sub'}, dimensions={0} | all-to-all | bytes 262144 | tf_op jit(solution)/shard_map/all_to_all | solution.py:193
  38.0 0.6 %convert_reduce_fusion = f32[8,256]{1,0:T(8,128)} fusion(bf16[32,8,256]{2,1,0:T(8,128)(2,1)S(1)} %all_to_all.5), kind=kLoop, calls=%fused_computation | loop fusion | flops 129024 | bytes 139264 | tf_op jit(solution)/shard_map/reduce_sum | solution.py:196
Async XLA Ops:
  0.0 10.0 %collective-permute-start.2 = (bf16[270,1152]{1,0:T(8,128)(2,1)}, bf16[270,1152]{1,0:T(8,128)(2,1)S(1)}, u32[]{:S(2)}, u32[]{:S(2)}) collective-permute-start(bf16[270,1152]{1,0:T(8,128)(2,1)} %bitcast.9), channel_id=1, source_target_pairs={{0,4},{4,0},{1,5},{5,1},{2,6},{6,2},{3,7},{7,3},{8,12},{12,8},{9,1... | collective-permute-start | bytes 1866248 | tf_op jit(solution)/shard_map/ppermute | solution.py:137
  0.5 11.4 %collective-permute-start.1 = (bf16[270,1152]{1,0:T(8,128)(2,1)}, bf16[270,1152]{1,0:T(8,128)(2,1)S(1)}, u32[]{:S(2)}, u32[]{:S(2)}) collective-permute-start(bf16[270,1152]{1,0:T(8,128)(2,1)} %bitcast.10), channel_id=1, source_target_pairs={{0,1},{1,0},{2,3},{3,2},{5,6},{6,5},{4,8},{8,4},{7,11},{11,7},{9,1... | collective-permute-start | bytes 1866248 | tf_op jit(solution)/shard_map/ppermute | solution.py:137
  3.1 10.6 %collective-permute-start = (bf16[270,1152]{1,0:T(8,128)(2,1)}, bf16[270,1152]{1,0:T(8,128)(2,1)S(1)}, u32[]{:S(2)}, u32[]{:S(2)}) collective-permute-start(bf16[270,1152]{1,0:T(8,128)(2,1)} %bitcast.11), channel_id=1, source_target_pairs={{1,2},{2,1},{5,9},{9,5},{6,10},{10,6},{13,14},{14,13},{12,16},{16,... | collective-permute-start | bytes 1866248 | tf_op jit(solution)/shard_map/ppermute | solution.py:137
  3.8 11.7 %collective-permute-start.3 = (bf16[270,1152]{1,0:T(8,128)(2,1)}, bf16[270,1152]{1,0:T(8,128)(2,1)S(1)}, u32[]{:S(2)}, u32[]{:S(2)}) collective-permute-start(bf16[270,1152]{1,0:T(8,128)(2,1)} %bitcast.12), channel_id=1, source_target_pairs={{4,5},{5,4},{6,7},{7,6},{8,9},{9,8},{10,11},{11,10},{13,17},{17,13... | collective-permute-start | bytes 1866248 | tf_op jit(solution)/shard_map/ppermute | solution.py:137

commit v4 on v3

--- a/solution.py
+++ b/solution.py
@@ -49,25 +49,49 @@
     return swaps, sources
 
 
-def margin_product(number, me, source_ref, index_ref, count_ref, values, coupling_ref, picked):
-    source = source_ref[me, number]
-    direction = jnp.maximum(source, 0)
-    live = count_ref[0, 0, direction]
-    for slot in range(index_ref.shape[-1]):
-        place = index_ref[0, 0, direction, slot]
+def packing(panels, slots):
+    bits, count_bits = (panels - 1).bit_length(), slots.bit_length()
+    assert slots * bits + count_bits + 2 < 32
+    return bits, count_bits
+
+
+def margin_product(number, plan_ref, values, coupling_ref, picked):
+    slots = picked.shape[1] // PANEL
+    bits, count_bits = packing(values.shape[1] // PANEL, slots)
+    plan = plan_ref[0, number]
+    direction = plan & 3
+    live = (plan >> 2) & (2**count_bits - 1)
+    for slot in range(slots):
+        place = (plan >> (2 + count_bits + slot * bits)) & (2**bits - 1)
         panel = values[:, pl.ds(pl.multiple_of(place * PANEL, PANEL), PANEL)]
         alive = jnp.where(slot < live, 1.0, 0.0).astype(BF16)
         picked[:, slot * PANEL : (slot + 1) * PANEL] = panel * alive
     return jnp.dot(picked[...], coupling_ref[direction], preferred_element_type=F32)
 
 
+def write_plans(source_ref, index_ref, count_ref, panels, plan_ref):
+    slots = index_ref.shape[-1]
+    bits, count_bits = packing(panels, slots)
+    me = place_of()
+    at = lax.broadcasted_iota(jnp.int32, plan_ref.shape, 1)
+    plans = jnp.zeros(plan_ref.shape, jnp.int32)
+    for number in range(source_ref.shape[1]):
+        source = source_ref[me, number]
+        direction = jnp.maximum(source, 0)
+        plan = direction + jnp.where(source < 0, 0, count_ref[0, 0, direction]) * 4
+        for slot in range(slots):
+            plan += index_ref[0, 0, direction, slot] << (2 + count_bits + slot * bits)
+        plans = jnp.where(at == number, plan, plans)
+    plan_ref[...] = plans
+
+
 def place_of():
     return lax.axis_index("grp") * lax.axis_size("sub") + lax.axis_index("sub")
 
 
 def early_kernel(
-    owner_ref, basis_hbm, inverse_hbm, coupling_hbm, stiffness_hbm,
-    first_ref, table_ref, turned_ref, inverse_ref, coupling_ref, stiffness_ref,
+    source_ref, index_ref, count_ref, owner_ref, basis_hbm, inverse_hbm, coupling_hbm, stiffness_hbm,
+    plan_ref, first_ref, table_ref, turned_ref, inverse_ref, coupling_ref, stiffness_ref,
     basis_ref, arrived,
 ):
     copies = [
@@ -83,6 +107,7 @@
     ]
     for copy in copies:
         copy.start()
+    write_plans(source_ref, index_ref, count_ref, basis_ref.shape[1] // PANEL, plan_ref)
     places = lax.broadcasted_iota(jnp.int32, table_ref.shape, 0)
     table = (owner_ref[0] == places).astype(F32)
     table_ref[...] = table.astype(BF16)
@@ -94,25 +119,18 @@
     copies[3].wait()
 
 
-def margin_kernel(number, source_ref, index_ref, count_ref, values, coupling_ref, *refs):
+def margin_kernel(number, plan_ref, values, coupling_ref, *refs):
     *so_far, out_ref, picked = refs
-    product = margin_product(
-        number, place_of(), source_ref, index_ref, count_ref, values, coupling_ref, picked
-    )
+    product = margin_product(number, plan_ref, values, coupling_ref, picked)
     out_ref[...] = so_far[0][...] + product if so_far else product
 
 
-def last_kernel(
-    numbers, scale, source_ref, index_ref, count_ref, table_ref, turned_ref, first_ref, so_far, *refs
-):
+def last_kernel(numbers, scale, plan_ref, table_ref, turned_ref, first_ref, so_far, *refs):
     arrived = refs[: len(numbers)]
     coupling_ref, inverse_ref, stiffness_ref, out_ref, picked, margin = refs[len(numbers) :]
     columns = margin.shape[0]
-    me = place_of()
     for at, (number, values) in enumerate(zip(numbers, arrived)):
-        product = margin_product(
-            number, me, source_ref, index_ref, count_ref, values, coupling_ref, picked
-        )
+        product = margin_product(number, plan_ref, values, coupling_ref, picked)
         margin[...] = (so_far if at == 0 else margin)[...] + product
     extension = (
         first_ref[...]
@@ -144,16 +162,17 @@
     room = 8 * 2**20 + 4 * columns_all**2
     params = pltpu.CompilerParams(vmem_limit_bytes=room)
     whole = jax.ShapeDtypeStruct((columns, rows), F32)
-    first, table, turned, inverse, coupling, stiffness = pl.pallas_call(
+    plan, first, table, turned, inverse, coupling, stiffness = pl.pallas_call(
         early_kernel,
         out_shape=(
+            jax.ShapeDtypeStruct((8, 128), jnp.int32),
             whole,
             jax.ShapeDtypeStruct((columns_all, columns), BF16),
             jax.ShapeDtypeStruct((columns, columns_all), BF16),
             *(jax.ShapeDtypeStruct(a.shape, BF16) for a in (inverse, coupling, stiffness)),
         ),
-        in_specs=[VMEM] + [HBM] * 4,
-        out_specs=(VMEM,) * 6,
+        in_specs=[SMEM] * 3 + [VMEM] + [HBM] * 4,
+        out_specs=(VMEM,) * 7,
         scratch_shapes=[
             pltpu.VMEM((columns, rows), BF16), pltpu.SemaphoreType.DMA((4,))
         ],
@@ -161,26 +180,26 @@
             flops=2 * columns * rows * rows, bytes_accessed=26 * 2**20, transcendentals=0
         ),
         compiler_params=pltpu.CompilerParams(vmem_limit_bytes=room + 16 * 2**20),
-    )(*stay(owner_map, basis, inverse, coupling, stiffness))
+    )(*tables, *stay(owner_map, basis, inverse, coupling, stiffness))
     margin = ()
     for number in MIDDLE:
         margin = (
             pl.pallas_call(
                 lambda *refs, number=number: margin_kernel(number, *refs),
                 out_shape=whole,
-                in_specs=[SMEM] * 3 + [VMEM] * (2 + len(margin)),
+                in_specs=[VMEM] * (3 + len(margin)),
                 out_specs=VMEM,
                 scratch_shapes=[picked],
                 cost_estimate=pl.CostEstimate(
                     flops=step, bytes_accessed=3 * 2**20, transcendentals=0
                 ),
                 compiler_params=params,
-            )(*tables, arrivals[number], coupling, *margin),
+            )(plan, arrivals[number], coupling, *margin),
         )
     contributions = pl.pallas_call(
         lambda *refs: last_kernel(LATE, scale, *refs),
         out_shape=jax.ShapeDtypeStruct((columns_all, columns_all), BF16),
-        in_specs=[SMEM] * 3 + [VMEM] * (7 + len(LATE)),
+        in_specs=[VMEM] * (8 + len(LATE)),
         out_specs=VMEM,
         scratch_shapes=[picked, pltpu.VMEM((columns, rows), F32)],
         cost_estimate=pl.CostEstimate(
@@ -189,7 +208,7 @@
             transcendentals=0,
         ),
         compiler_params=params,
-    )(*tables, table, turned, first, *margin, *(arrivals[n] for n in LATE), coupling, inverse, stiffness)
+    )(plan, table, turned, first, *margin, *(arrivals[n] for n in LATE), coupling, inverse, stiffness)
     parts = lax.all_to_all(
         contributions.reshape(blocks, OWN, columns_all), ("grp", "sub"), 0, 0, tiled=True
     )

time: 39.1 us -> 37.5 us (0.959)
  Pallas kernels: 15.2 us -> 12.1 us
  blocking collectives: 18.2 us -> 19.3 us
  waiting for transfers between devices: 0.19 us -> 0.75 us
    pallas_call x3, Pallas kernels: 5.18 us -> 2.59 us  [shards(): pl.pallas_call(lambda *refs, number=number: margin_kernel(number, *refs),...]
    all_to_all x1, blocking collectives: 18.2 us -> 19.3 us  [shards(): lax.all_to_all(contributions.reshape(blocks, OWN, columns_all), ('grp', '...]
    pallas_call x1, Pallas kernels: 4.44 us -> 3.65 us  [shards(): pl.pallas_call(lambda *refs: last_kernel(LATE, scale, *refs), out_shape=j...]
    ppermute x4, waiting for transfers between devices: 0.19 us -> 0.75 us  [shards(): arrivals[number] = lax.ppermute(basis, ('grp', 'sub'), swaps[number])]
  transfers between devices with their start and end apart: 4 -> 4, of which waited for: 1 -> 1; matrix products, arithmetic and copies ran while one was open for 0% -> 0% of each run, Pallas kernels for 28% -> 23%
where the time goes in v4:
time: 37.5 us; the launch traced here: 37.3 us
  blocking collectives  19.3 us (51%)
  Pallas kernels  12.1 us (32%)
  starting transfers between devices  4.44 us (12%)
  waiting for transfers between devices  0.75 us (2%)
  other arithmetic  0.63 us (2%)
    all_to_all x1, blocking collectives, shards(): lax.all_to_all(contributions.reshape(blocks, OWN, columns_all), ('grp', '...  19.3 us
    pallas_call x1, Pallas kernels, shards(): pl.pallas_call(early_kernel, out_shape=(jax.ShapeDtypeStruct((8, 128), jn...  5.84 us
    ppermute x4, starting transfers between devices, shards(): arrivals[number] = lax.ppermute(basis, ('grp', 'sub'), swaps[number])  4.44 us
    pallas_call x1, Pallas kernels, shards(): pl.pallas_call(lambda *refs: last_kernel(LATE, scale, *refs), out_shape=j...  3.65 us
    pallas_call x3, Pallas kernels, shards(): pl.pallas_call(lambda *refs, number=number: margin_kernel(number, *refs),...  2.59 us
    ppermute x4, waiting for transfers between devices, shards(): arrivals[number] = lax.ppermute(basis, ('grp', 'sub'), swaps[number])  0.75 us
  transfers between devices with their start and end apart: 4, of which 1 were waited for; matrix products, arithmetic and copies ran while one was open for 0% of the time, Pallas kernels for 23%

profile of v4, /device:TPU:0, one launch (start us, length us, event | category | flops | bytes accessed | tf_op | source)
XLA Modules:
  0.0 37.3 jit_solution(6539977498170777409)
XLA Ops:
  0.0 0.5 %collective-permute-start.2 = (bf16[270,1152]{1,0:T(8,128)(2,1)}, bf16[270,1152]{1,0:T(8,128)(2,1)S(1)}, u32[]{:S(2)}, u32[]{:S(2)}) collective-permute-start(bf16[270,1152]{1,0:T(8,128)(2,1)} %bitcast.9), channel_id=1, source_target_pairs={{0,4},{4,0},{1,5},{5,1},{2,6},{6,2},{3,7},{7,3},{8,12},{12,8},{9,1... | collective-permute-start | bytes 1866248 | tf_op jit(solution)/shard_map/ppermute | solution.py:155
  0.5 2.6 %collective-permute-start.1 = (bf16[270,1152]{1,0:T(8,128)(2,1)}, bf16[270,1152]{1,0:T(8,128)(2,1)S(1)}, u32[]{:S(2)}, u32[]{:S(2)}) collective-permute-start(bf16[270,1152]{1,0:T(8,128)(2,1)} %bitcast.10), channel_id=1, source_target_pairs={{0,1},{1,0},{2,3},{3,2},{5,6},{6,5},{4,8},{8,4},{7,11},{11,7},{9,1... | collective-permute-start | bytes 1866248 | tf_op jit(solution)/shard_map/ppermute | solution.py:155
  3.1 0.7 %collective-permute-start = (bf16[270,1152]{1,0:T(8,128)(2,1)}, bf16[270,1152]{1,0:T(8,128)(2,1)S(1)}, u32[]{:S(2)}, u32[]{:S(2)}) collective-permute-start(bf16[270,1152]{1,0:T(8,128)(2,1)} %bitcast.11), channel_id=1, source_target_pairs={{1,2},{2,1},{5,9},{9,5},{6,10},{10,6},{13,14},{14,13},{12,16},{16,... | collective-permute-start | bytes 1866248 | tf_op jit(solution)/shard_map/ppermute | solution.py:155
  3.8 0.7 %collective-permute-start.3 = (bf16[270,1152]{1,0:T(8,128)(2,1)}, bf16[270,1152]{1,0:T(8,128)(2,1)S(1)}, u32[]{:S(2)}, u32[]{:S(2)}) collective-permute-start(bf16[270,1152]{1,0:T(8,128)(2,1)} %bitcast.12), channel_id=1, source_target_pairs={{4,5},{5,4},{6,7},{7,6},{8,9},{9,8},{10,11},{11,10},{13,17},{17,13... | collective-permute-start | bytes 1866248 | tf_op jit(solution)/shard_map/ppermute | solution.py:155
  4.5 5.8 %shard_map.82 = (s32[8,128]{1,0:T(8,128)S(1)}, f32[270,1152]{1,0:T(8,128)S(1)}, bf16[256,270]{1,0:T(8,128)(2,1)S(1)}, bf16[270,256]{1,0:T(8,128)(2,1)S(1)}, bf16...) custom-call(s32[32,4]{1,0:T(8,128)} %constant.4.clone.source_ref, ...), custom_call_target="tpu_custom_call" | custom-call | flops 716636160 | bytes 27262976 | tf_op jit(solution)/shard_map/pallas_call | solution.py:165
  10.3 0.0 collective-permute-done.2.refs_1_
  10.3 0.9 %shard_map.83.refs_3_ = f32[270,1152]{1,0:T(8,128)S(1)} custom-call(s32[8,128]{1,0:T(8,128)S(1)} %get-tuple-element.12.refs_0_, bf16[270,1152]{1,0:T(8,128)(2,1)S(1)} %collective-permute-done.2.refs_1_, bf16[4,768,1152]{2,1,0:T(8,128)(2,1)S(1)} %get-tuple-element.16.refs_2_.refs_6_), custom_call_target="tpu_custom_call" | custom-call | flops 477757440 | bytes 3145728 | tf_op jit(solution)/shard_map/pallas_call | solution.py:187
  11.2 0.7 %collective-permute-done.1.refs_1_ = bf16[270,1152]{1,0:T(8,128)(2,1)S(1)} collective-permute-done((bf16[270,1152]{1,0:T(8,128)(2,1)}, bf16[270,1152]{1,0:T(8,128)(2,1)S(1)}, u32[]{:S(2)}, u32[]{:S(2)}) %collective-permute-start.1) | collective-permute-done | bytes 622112 | tf_op jit(solution)/shard_map/ppermute | solution.py:155
  11.9 0.8 %shard_map.84.refs_3_ = f32[270,1152]{1,0:T(8,128)S(1)} custom-call(s32[8,128]{1,0:T(8,128)S(1)} %get-tuple-element.12.refs_0_, bf16[270,1152]{1,0:T(8,128)(2,1)S(1)} %collective-permute-done.1.refs_1_, bf16[4,768,1152]{2,1,0:T(8,128)(2,1)S(1)} %get-tuple-element.16.refs_2_.refs_6_, f32[270,1152]{1,0:T(8,128)S(1)} %shard_map.83.refs_3_), custom_call_target="tpu_custom_call" | custom-call | flops 477757440 | bytes 3145728 | tf_op jit(solution)/shard_map/pallas_call | solution.py:187
  12.8 0.0 collective-permute-done.refs_1_
  12.8 0.9 %shard_map.85.refs_4_ = f32[270,1152]{1,0:T(8,128)S(1)} custom-call(s32[8,128]{1,0:T(8,128)S(1)} %get-tuple-element.12.refs_0_, bf16[270,1152]{1,0:T(8,128)(2,1)S(1)} %collective-permute-done.refs_1_, bf16[4,768,1152]{2,1,0:T(8,128)(2,1)S(1)} %get-tuple-element.16.refs_2_.refs_6_, f32[270,1152]{1,0:T(8,128)S(1)} %shard_map.84.refs_3_), custom_call_target="tpu_custom_call" | custom-call | flops 477757440 | bytes 3145728 | tf_op jit(solution)/shard_map/pallas_call | solution.py:187
  13.7 0.0 collective-permute-done.3.refs_5_
  13.7 3.6 %shard_map.86 = bf16[256,256]{1,0:T(8,128)(2,1)S(1)} custom-call(s32[8,128]{1,0:T(8,128)S(1)} %get-tuple-element.12.refs_0_, bf16[256,270]{1,0:T(8,128)(2,1)S(1)} %get-tuple-element.13.refs_1_, bf16[270,256]{1,0:T(8,128)(2,1)S(1)} %get-tuple-element.14.refs_2_, f32[270,1152]{1,0:T(8,128)S(1)} %get-tuple-element.15.refs_3_, ...), custom_call_target="tpu_custom_call" | custom-call | flops 2078991360 | bytes 12582912 | tf_op jit(solution)/shard_map/pallas_call | solution.py:199
  17.3 19.3 %all_to_all.5 = bf16[32,8,256]{2,1,0:T(8,128)(2,1)S(1)} all-to-all(bf16[32,8,256]{2,1,0:T(8,128)(2,1)S(1)} %bitcast.5), channel_id=1, replica_groups=mesh['grp'=8,'sub'=4] {'grp','sub'}, dimensions={0} | all-to-all | bytes 262144 | tf_op jit(solution)/shard_map/all_to_all | solution.py:212
  36.7 0.6 %convert_reduce_fusion = f32[8,256]{1,0:T(8,128)} fusion(bf16[32,8,256]{2,1,0:T(8,128)(2,1)S(1)} %all_to_all.5), kind=kLoop, calls=%fused_computation | loop fusion | flops 129024 | bytes 139264 | tf_op jit(solution)/shard_map/reduce_sum | solution.py:215
Async XLA Ops:
  0.0 10.3 %collective-permute-start.2 = (bf16[270,1152]{1,0:T(8,128)(2,1)}, bf16[270,1152]{1,0:T(8,128)(2,1)S(1)}, u32[]{:S(2)}, u32[]{:S(2)}) collective-permute-start(bf16[270,1152]{1,0:T(8,128)(2,1)} %bitcast.9), channel_id=1, source_target_pairs={{0,4},{4,0},{1,5},{5,1},{2,6},{6,2},{3,7},{7,3},{8,12},{12,8},{9,1... | collective-permute-start | bytes 1866248 | tf_op jit(solution)/shard_map/ppermute | solution.py:155
  0.5 11.4 %collective-permute-start.1 = (bf16[270,1152]{1,0:T(8,128)(2,1)}, bf16[270,1152]{1,0:T(8,128)(2,1)S(1)}, u32[]{:S(2)}, u32[]{:S(2)}) collective-permute-start(bf16[270,1152]{1,0:T(8,128)(2,1)} %bitcast.10), channel_id=1, source_target_pairs={{0,1},{1,0},{2,3},{3,2},{5,6},{6,5},{4,8},{8,4},{7,11},{11,7},{9,1... | collective-permute-start | bytes 1866248 | tf_op jit(solution)/shard_map/ppermute | solution.py:155
  3.1 9.7 %collective-permute-start = (bf16[270,1152]{1,0:T(8,128)(2,1)}, bf16[270,1152]{1,0:T(8,128)(2,1)S(1)}, u32[]{:S(2)}, u32[]{:S(2)}) collective-permute-start(bf16[270,1152]{1,0:T(8,128)(2,1)} %bitcast.11), channel_id=1, source_target_pairs={{1,2},{2,1},{5,9},{9,5},{6,10},{10,6},{13,14},{14,13},{12,16},{16,... | collective-permute-start | bytes 1866248 | tf_op jit(solution)/shard_map/ppermute | solution.py:155
  3.8 9.9 %collective-permute-start.3 = (bf16[270,1152]{1,0:T(8,128)(2,1)}, bf16[270,1152]{1,0:T(8,128)(2,1)S(1)}, u32[]{:S(2)}, u32[]{:S(2)}) collective-permute-start(bf16[270,1152]{1,0:T(8,128)(2,1)} %bitcast.12), channel_id=1, source_target_pairs={{4,5},{5,4},{6,7},{7,6},{8,9},{9,8},{10,11},{11,10},{13,17},{17,13... | collective-permute-start | bytes 1866248 | tf_op jit(solution)/shard_map/ppermute | solution.py:155

commit v5 on v4

--- a/solution.py
+++ b/solution.py
@@ -10,7 +10,7 @@
 OWN = 8
 F32 = jnp.float32
 BF16 = jnp.bfloat16
-MIDDLE, LATE = (3, 0, 1), (2,)
+FIRST, MIDDLE, LATE = (3, 0), 1, 2
 ORDER = (0, 1, 2, 3)
 VMEM = pl.BlockSpec(memory_space=pltpu.VMEM)
 SMEM = pl.BlockSpec(memory_space=pltpu.SMEM)
@@ -55,18 +55,27 @@
     return bits, count_bits
 
 
-def margin_product(number, plan_ref, values, coupling_ref, picked):
-    slots = picked.shape[1] // PANEL
-    bits, count_bits = packing(values.shape[1] // PANEL, slots)
+def unpacked(number, plan_ref, panels, slots):
+    bits, count_bits = packing(panels, slots)
     plan = plan_ref[0, number]
-    direction = plan & 3
-    live = (plan >> 2) & (2**count_bits - 1)
-    for slot in range(slots):
-        place = (plan >> (2 + count_bits + slot * bits)) & (2**bits - 1)
+    places = [(plan >> (2 + count_bits + slot * bits)) & (2**bits - 1) for slot in range(slots)]
+    return plan & 3, (plan >> 2) & (2**count_bits - 1), places
+
+
+def side_by_side(values, live, places):
+    panels = []
+    for slot, place in enumerate(places):
         panel = values[:, pl.ds(pl.multiple_of(place * PANEL, PANEL), PANEL)]
-        alive = jnp.where(slot < live, 1.0, 0.0).astype(BF16)
-        picked[:, slot * PANEL : (slot + 1) * PANEL] = panel * alive
-    return jnp.dot(picked[...], coupling_ref[direction], preferred_element_type=F32)
+        panels.append(panel * jnp.where(slot < live, 1.0, 0.0).astype(BF16))
+    return jnp.concatenate(panels, axis=1)
+
+
+def margin_product(number, plan_ref, values, coupling_ref):
+    panels, slots = (width // PANEL for width in (values.shape[1], coupling_ref.shape[1]))
+    direction, live, places = unpacked(number, plan_ref, panels, slots)
+    return jnp.dot(
+        side_by_side(values, live, places), coupling_ref[direction], preferred_element_type=F32
+    )
 
 
 def write_plans(source_ref, index_ref, count_ref, panels, plan_ref):
@@ -91,19 +100,17 @@
 
 def early_kernel(
     source_ref, index_ref, count_ref, owner_ref, basis_hbm, inverse_hbm, coupling_hbm, stiffness_hbm,
-    plan_ref, first_ref, table_ref, turned_ref, inverse_ref, coupling_ref, stiffness_ref,
+    plan_ref, first_ref, table_ref, turned_ref, through_ref, inverse_ref, coupling_ref, stiffness_ref,
     basis_ref, arrived,
 ):
+    last = jnp.maximum(source_ref[place_of(), LATE], 0)
+    pairs = [(inverse_hbm, inverse_ref)]
+    pairs += [(coupling_hbm.at[last ^ way], coupling_ref.at[last ^ way]) for way in range(4)]
+    pairs[2:2] = [(basis_hbm, basis_ref)]
+    pairs += [(stiffness_hbm, stiffness_ref)]
     copies = [
         pltpu.make_async_copy(source, target, arrived.at[at])
-        for at, (source, target) in enumerate(
-            (
-                (basis_hbm, basis_ref),
-                (inverse_hbm, inverse_ref),
-                (coupling_hbm, coupling_ref),
-                (stiffness_hbm, stiffness_ref),
-            )
-        )
+        for at, (source, target) in enumerate(pairs)
     ]
     for copy in copies:
         copy.start()
@@ -114,28 +121,49 @@
     turned_ref[...] = table.T.astype(BF16)
     copies[0].wait()
     copies[1].wait()
+    depth = through_ref.shape[0]
+    part = 2 * PANEL if depth % (2 * PANEL) == 0 else PANEL
+    for start in range(0, depth, part):
+        through_ref[start : start + part] = jnp.dot(
+            coupling_ref[last, start : start + part], inverse_ref[...], preferred_element_type=F32
+        ).astype(BF16)
+    copies[2].wait()
     first_ref[...] = jnp.dot(basis_ref[...], inverse_ref[...], preferred_element_type=F32)
-    copies[2].wait()
-    copies[3].wait()
+    for copy in copies[3:]:
+        copy.wait()
 
 
 def margin_kernel(number, plan_ref, values, coupling_ref, *refs):
-    *so_far, out_ref, picked = refs
-    product = margin_product(number, plan_ref, values, coupling_ref, picked)
+    *so_far, out_ref = refs
+    product = margin_product(number, plan_ref, values, coupling_ref)
     out_ref[...] = so_far[0][...] + product if so_far else product
 
 
-def last_kernel(numbers, scale, plan_ref, table_ref, turned_ref, first_ref, so_far, *refs):
-    arrived = refs[: len(numbers)]
-    coupling_ref, inverse_ref, stiffness_ref, out_ref, picked, margin = refs[len(numbers) :]
-    columns = margin.shape[0]
-    for at, (number, values) in enumerate(zip(numbers, arrived)):
-        product = margin_product(number, plan_ref, values, coupling_ref, picked)
-        margin[...] = (so_far if at == 0 else margin)[...] + product
-    extension = (
-        first_ref[...]
-        + jnp.dot(margin[...].astype(BF16), inverse_ref[...], preferred_element_type=F32)
-    ).astype(BF16)
+def partial_kernel(number, plan_ref, values, coupling_ref, so_far, first_ref, inverse_ref, out_ref):
+    margin = so_far[...] + margin_product(number, plan_ref, values, coupling_ref)
+    out_ref[...] = first_ref[...] + jnp.dot(
+        margin.astype(BF16), inverse_ref[...], preferred_element_type=F32
+    )
+
+
+def last_kernel(
+    scale, plan_ref, table_ref, turned_ref, partial_ref, values, through_ref, stiffness_ref,
+    out_ref, extension_ref,
+):
+    panels, slots = (width // PANEL for width in (values.shape[1], through_ref.shape[0]))
+    _, live, places = unpacked(LATE, plan_ref, panels, slots)
+
+    @pl.when(live == 0)
+    def _():
+        extension_ref[...] = partial_ref[...].astype(BF16)
+
+    @pl.when(live > 0)
+    def _():
+        picked = side_by_side(values, live, places)
+        product = jnp.dot(picked, through_ref[...], preferred_element_type=F32)
+        extension_ref[...] = (partial_ref[...] + product).astype(BF16)
+
+    extension = extension_ref[...]
     projected = jnp.dot(extension, stiffness_ref[...], preferred_element_type=F32).astype(BF16)
     coarse = lax.dot_general(
         projected, extension, (((1,), (1,)), ((), ())), preferred_element_type=F32
@@ -157,58 +185,67 @@
     tables = stay(jnp.asarray(sources), panel_index, panel_count)
     scale = float(rows * columns) ** -0.5
     slots_wide = coupling.shape[1]
-    picked = pltpu.VMEM((columns, slots_wide), BF16)
     step = 2 * columns * slots_wide * rows
     room = 8 * 2**20 + 4 * columns_all**2
     params = pltpu.CompilerParams(vmem_limit_bytes=room)
     whole = jax.ShapeDtypeStruct((columns, rows), F32)
-    plan, first, table, turned, inverse, coupling, stiffness = pl.pallas_call(
+    plan, first, table, turned, through, inverse, coupling, stiffness = pl.pallas_call(
         early_kernel,
         out_shape=(
             jax.ShapeDtypeStruct((8, 128), jnp.int32),
             whole,
             jax.ShapeDtypeStruct((columns_all, columns), BF16),
             jax.ShapeDtypeStruct((columns, columns_all), BF16),
+            jax.ShapeDtypeStruct((slots_wide, rows), BF16),
             *(jax.ShapeDtypeStruct(a.shape, BF16) for a in (inverse, coupling, stiffness)),
         ),
         in_specs=[SMEM] * 3 + [VMEM] + [HBM] * 4,
-        out_specs=(VMEM,) * 7,
+        out_specs=(VMEM,) * 8,
         scratch_shapes=[
-            pltpu.VMEM((columns, rows), BF16), pltpu.SemaphoreType.DMA((4,))
+            pltpu.VMEM((columns, rows), BF16), pltpu.SemaphoreType.DMA((7,))
         ],
         cost_estimate=pl.CostEstimate(
-            flops=2 * columns * rows * rows, bytes_accessed=26 * 2**20, transcendentals=0
+            flops=2 * (columns + slots_wide) * rows * rows, bytes_accessed=26 * 2**20, transcendentals=0
         ),
         compiler_params=pltpu.CompilerParams(vmem_limit_bytes=room + 16 * 2**20),
     )(*tables, *stay(owner_map, basis, inverse, coupling, stiffness))
     margin = ()
-    for number in MIDDLE:
+    for number in FIRST:
         margin = (
             pl.pallas_call(
                 lambda *refs, number=number: margin_kernel(number, *refs),
                 out_shape=whole,
                 in_specs=[VMEM] * (3 + len(margin)),
                 out_specs=VMEM,
-                scratch_shapes=[picked],
                 cost_estimate=pl.CostEstimate(
                     flops=step, bytes_accessed=3 * 2**20, transcendentals=0
                 ),
                 compiler_params=params,
             )(plan, arrivals[number], coupling, *margin),
         )
+    partial = pl.pallas_call(
+        lambda *refs: partial_kernel(MIDDLE, *refs),
+        out_shape=whole,
+        in_specs=[VMEM] * 6,
+        out_specs=VMEM,
+        cost_estimate=pl.CostEstimate(
+            flops=step + 2 * columns * rows * rows, bytes_accessed=6 * 2**20, transcendentals=0
+        ),
+        compiler_params=params,
+    )(plan, arrivals[MIDDLE], coupling, *margin, first, inverse)
     contributions = pl.pallas_call(
-        lambda *refs: last_kernel(LATE, scale, *refs),
+        lambda *refs: last_kernel(scale, *refs),
         out_shape=jax.ShapeDtypeStruct((columns_all, columns_all), BF16),
-        in_specs=[VMEM] * (8 + len(LATE)),
+        in_specs=[VMEM] * 7,
         out_specs=VMEM,
-        scratch_shapes=[picked, pltpu.VMEM((columns, rows), F32)],
+        scratch_shapes=[pltpu.VMEM((columns, rows), BF16)],
         cost_estimate=pl.CostEstimate(
-            flops=step * len(LATE) + 2 * columns * rows * (2 * rows + columns),
-            bytes_accessed=12 * 2**20,
+            flops=step + 2 * columns * rows * (rows + columns),
+            bytes_accessed=8 * 2**20,
             transcendentals=0,
         ),
         compiler_params=params,
-    )(plan, table, turned, first, *margin, *(arrivals[n] for n in LATE), coupling, inverse, stiffness)
+    )(plan, table, turned, partial, arrivals[LATE], through, stiffness)
     parts = lax.all_to_all(
         contributions.reshape(blocks, OWN, columns_all), ("grp", "sub"), 0, 0, tiled=True
     )

time: 37.5 us -> 36.7 us (0.979)
  waiting for transfers between devices: 0.75 us -> 0.01 us
  Pallas kernels: 12.1 us -> 12.8 us
  blocking collectives: 19.3 us -> 18.6 us
    pallas_call x1, Pallas kernels: 5.84 us -> 7.16 us  [shards(): pl.pallas_call(early_kernel, out_shape=(jax.ShapeDtypeStruct((8, 128), jn...]
    pallas_call x3 -> x2, Pallas kernels: 2.59 us -> 1.64 us  [shards(): pl.pallas_call(lambda *refs, number=number: margin_kernel(number, *refs),...]
    all_to_all x1, blocking collectives: 19.3 us -> 18.6 us  [shards(): lax.all_to_all(contributions.reshape(blocks, OWN, columns_all), ('grp', '...]
    ppermute x4, waiting for transfers between devices: 0.75 us -> 0.01 us  [shards(): arrivals[number] = lax.ppermute(basis, ('grp', 'sub'), swaps[number])]
    pallas_call x1 -> x2, Pallas kernels: 3.65 us -> 3.95 us  [the longest x1 2.16 us: shards(): pl.pallas_call(lambda *refs: last_kernel(scale, *refs), out_shape=jax.Sha...]
  transfers between devices with their start and end apart: 4 -> 4, of which waited for: 1 -> 0; matrix products, arithmetic and copies ran while one was open for 0% -> 0% of each run, Pallas kernels for 23% -> 29%
where the time goes in v5:
time: 36.7 us; the launch traced here: 36.5 us
  blocking collectives  18.6 us (51%)
  Pallas kernels  12.8 us (35%)
  starting transfers between devices  4.44 us (12%)
  other arithmetic  0.63 us (2%)
    all_to_all x1, blocking collectives, shards(): lax.all_to_all(contributions.reshape(blocks, OWN, columns_all), ('grp', '...  18.6 us
    pallas_call x1, Pallas kernels, shards(): pl.pallas_call(early_kernel, out_shape=(jax.ShapeDtypeStruct((8, 128), jn...  7.16 us
    ppermute x4, starting transfers between devices, shards(): arrivals[number] = lax.ppermute(basis, ('grp', 'sub'), swaps[number])  4.44 us
    pallas_call x1, Pallas kernels, shards(): pl.pallas_call(lambda *refs: last_kernel(scale, *refs), out_shape=jax.Sha...  2.16 us
    pallas_call x1, Pallas kernels, shards(): pl.pallas_call(lambda *refs: partial_kernel(MIDDLE, *refs), out_shape=who...  1.79 us
    pallas_call x2, Pallas kernels, shards(): pl.pallas_call(lambda *refs, number=number: margin_kernel(number, *refs),...  1.64 us
  transfers between devices with their start and end apart: 4, of which 0 were waited for; matrix products, arithmetic and copies ran while one was open for 0% of the time, Pallas kernels for 29%

profile of v5, /device:TPU:0, one launch (start us, length us, event | category | flops | bytes accessed | tf_op | source)
XLA Modules:
  0.0 36.5 jit_solution(402548366888783179)
XLA Ops:
  0.0 0.5 %collective-permute-start.2 = (bf16[270,1152]{1,0:T(8,128)(2,1)}, bf16[270,1152]{1,0:T(8,128)(2,1)S(1)}, u32[]{:S(2)}, u32[]{:S(2)}) collective-permute-start(bf16[270,1152]{1,0:T(8,128)(2,1)} %bitcast.9), channel_id=1, source_target_pairs={{0,4},{4,0},{1,5},{5,1},{2,6},{6,2},{3,7},{7,3},{8,12},{12,8},{9,1... | collective-permute-start | bytes 1866248 | tf_op jit(solution)/shard_map/ppermute | solution.py:183
  0.5 2.6 %collective-permute-start.1 = (bf16[270,1152]{1,0:T(8,128)(2,1)}, bf16[270,1152]{1,0:T(8,128)(2,1)S(1)}, u32[]{:S(2)}, u32[]{:S(2)}) collective-permute-start(bf16[270,1152]{1,0:T(8,128)(2,1)} %bitcast.10), channel_id=1, source_target_pairs={{0,1},{1,0},{2,3},{3,2},{5,6},{6,5},{4,8},{8,4},{7,11},{11,7},{9,1... | collective-permute-start | bytes 1866248 | tf_op jit(solution)/shard_map/ppermute | solution.py:183
  3.1 0.7 %collective-permute-start = (bf16[270,1152]{1,0:T(8,128)(2,1)}, bf16[270,1152]{1,0:T(8,128)(2,1)S(1)}, u32[]{:S(2)}, u32[]{:S(2)}) collective-permute-start(bf16[270,1152]{1,0:T(8,128)(2,1)} %bitcast.11), channel_id=1, source_target_pairs={{1,2},{2,1},{5,9},{9,5},{6,10},{10,6},{13,14},{14,13},{12,16},{16,... | collective-permute-start | bytes 1866248 | tf_op jit(solution)/shard_map/ppermute | solution.py:183
  3.8 0.7 %collective-permute-start.3 = (bf16[270,1152]{1,0:T(8,128)(2,1)}, bf16[270,1152]{1,0:T(8,128)(2,1)S(1)}, u32[]{:S(2)}, u32[]{:S(2)}) collective-permute-start(bf16[270,1152]{1,0:T(8,128)(2,1)} %bitcast.12), channel_id=1, source_target_pairs={{4,5},{5,4},{6,7},{7,6},{8,9},{9,8},{10,11},{11,10},{13,17},{17,13... | collective-permute-start | bytes 1866248 | tf_op jit(solution)/shard_map/ppermute | solution.py:183
  4.5 7.2 %shard_map.82 = (s32[8,128]{1,0:T(8,128)S(1)}, f32[270,1152]{1,0:T(8,128)S(1)}, bf16[256,270]{1,0:T(8,128)(2,1)S(1)}, bf16[270,256]{1,0:T(8,128)(2,1)S(1)}, bf16...) custom-call(s32[32,4]{1,0:T(8,128)} %constant.4.clone.source_ref, ...), custom_call_target="tpu_custom_call" | custom-call | flops 2755067904 | bytes 27262976 | tf_op jit(solution)/shard_map/pallas_call | solution.py:192
  11.6 0.0 collective-permute-done.2.refs_1_
  11.6 0.8 %shard_map.83.refs_3_ = f32[270,1152]{1,0:T(8,128)S(1)} custom-call(s32[8,128]{1,0:T(8,128)S(1)} %get-tuple-element.13.refs_0_, bf16[270,1152]{1,0:T(8,128)(2,1)S(1)} %collective-permute-done.2.refs_1_, bf16[4,768,1152]{2,1,0:T(8,128)(2,1)S(1)} %get-tuple-element.16.refs_2_), custom_call_target="tpu_custom_call" | custom-call | flops 477757440 | bytes 3145728 | tf_op jit(solution)/shard_map/pallas_call | solution.py:215
  12.5 0.0 collective-permute-done.1.refs_1_
  12.5 0.8 %shard_map.84.refs_3_ = f32[270,1152]{1,0:T(8,128)S(1)} custom-call(s32[8,128]{1,0:T(8,128)S(1)} %get-tuple-element.13.refs_0_, bf16[270,1152]{1,0:T(8,128)(2,1)S(1)} %collective-permute-done.1.refs_1_, bf16[4,768,1152]{2,1,0:T(8,128)(2,1)S(1)} %get-tuple-element.16.refs_2_, f32[270,1152]{1,0:T(8,128)S(1)} %shard_map.83.refs_3_), custom_call_target="tpu_custom_call" | custom-call | flops 477757440 | bytes 3145728 | tf_op jit(solution)/shard_map/pallas_call | solution.py:215
  13.3 0.0 collective-permute-done.refs_1_
  13.3 1.8 %shard_map.85.refs_3_ = f32[270,1152]{1,0:T(8,128)S(1)} custom-call(s32[8,128]{1,0:T(8,128)S(1)} %get-tuple-element.13.refs_0_, bf16[270,1152]{1,0:T(8,128)(2,1)S(1)} %collective-permute-done.refs_1_, bf16[4,768,1152]{2,1,0:T(8,128)(2,1)S(1)} %get-tuple-element.16.refs_2_, f32[270,1152]{1,0:T(8,128)S(1)} %shard_map.84.refs_3_, ...), custom_call_target="tpu_custom_call" | custom-call | flops 1194393600 | bytes 6291456 | tf_op jit(solution)/shard_map/pallas_call | solution.py:226
  15.1 0.0 collective-permute-done.3.refs_4_
  15.1 2.2 %shard_map.86 = bf16[256,256]{1,0:T(8,128)(2,1)S(1)} custom-call(s32[8,128]{1,0:T(8,128)S(1)} %get-tuple-element.13.refs_0_, bf16[256,270]{1,0:T(8,128)(2,1)S(1)} %get-tuple-element.14.refs_1_, bf16[270,256]{1,0:T(8,128)(2,1)S(1)} %get-tuple-element.15.refs_2_, f32[270,1152]{1,0:T(8,128)S(1)} %shard_map.85.refs_3_, ...), custom_call_target="tpu_custom_call" | custom-call | flops 1362355200 | bytes 8388608 | tf_op jit(solution)/shard_map/pallas_call | solution.py:236
  17.3 18.6 %all_to_all.5 = bf16[32,8,256]{2,1,0:T(8,128)(2,1)S(1)} all-to-all(bf16[32,8,256]{2,1,0:T(8,128)(2,1)S(1)} %bitcast.5), channel_id=1, replica_groups=mesh['grp'=8,'sub'=4] {'grp','sub'}, dimensions={0} | all-to-all | bytes 262144 | tf_op jit(solution)/shard_map/all_to_all | solution.py:249
  35.9 0.6 %convert_reduce_fusion = f32[8,256]{1,0:T(8,128)} fusion(bf16[32,8,256]{2,1,0:T(8,128)(2,1)S(1)} %all_to_all.5), kind=kLoop, calls=%fused_computation | loop fusion | flops 129024 | bytes 139264 | tf_op jit(solution)/shard_map/reduce_sum | solution.py:252
Async XLA Ops:
  0.0 11.6 %collective-permute-start.2 = (bf16[270,1152]{1,0:T(8,128)(2,1)}, bf16[270,1152]{1,0:T(8,128)(2,1)S(1)}, u32[]{:S(2)}, u32[]{:S(2)}) collective-permute-start(bf16[270,1152]{1,0:T(8,128)(2,1)} %bitcast.9), channel_id=1, source_target_pairs={{0,4},{4,0},{1,5},{5,1},{2,6},{6,2},{3,7},{7,3},{8,12},{12,8},{9,1... | collective-permute-start | bytes 1866248 | tf_op jit(solution)/shard_map/ppermute | solution.py:183
  0.5 12.0 %collective-permute-start.1 = (bf16[270,1152]{1,0:T(8,128)(2,1)}, bf16[270,1152]{1,0:T(8,128)(2,1)S(1)}, u32[]{:S(2)}, u32[]{:S(2)}) collective-permute-start(bf16[270,1152]{1,0:T(8,128)(2,1)} %bitcast.10), channel_id=1, source_target_pairs={{0,1},{1,0},{2,3},{3,2},{5,6},{6,5},{4,8},{8,4},{7,11},{11,7},{9,1... | collective-permute-start | bytes 1866248 | tf_op jit(solution)/shard_map/ppermute | solution.py:183
  3.1 10.3 %collective-permute-start = (bf16[270,1152]{1,0:T(8,128)(2,1)}, bf16[270,1152]{1,0:T(8,128)(2,1)S(1)}, u32[]{:S(2)}, u32[]{:S(2)}) collective-permute-start(bf16[270,1152]{1,0:T(8,128)(2,1)} %bitcast.11), channel_id=1, source_target_pairs={{1,2},{2,1},{5,9},{9,5},{6,10},{10,6},{13,14},{14,13},{12,16},{16,... | collective-permute-start | bytes 1866248 | tf_op jit(solution)/shard_map/ppermute | solution.py:183
  3.8 11.4 %collective-permute-start.3 = (bf16[270,1152]{1,0:T(8,128)(2,1)}, bf16[270,1152]{1,0:T(8,128)(2,1)S(1)}, u32[]{:S(2)}, u32[]{:S(2)}) collective-permute-start(bf16[270,1152]{1,0:T(8,128)(2,1)} %bitcast.12), channel_id=1, source_target_pairs={{4,5},{5,4},{6,7},{7,6},{8,9},{9,8},{10,11},{11,10},{13,17},{17,13... | collective-permute-start | bytes 1866248 | tf_op jit(solution)/shard_map/ppermute | solution.py:183
